TPU v7x, 32 devices: a whole 2x2x4 slice. The times are simulated.
32 devices in a mesh: beam: 8 (over z, x), tile: 4 (over y, core).
Axes of the slice: x: 2, y: 2, z: 4, core: 2. Of those that a mesh axis runs over, the one named last changes fastest.
Arguments:
- atom_counts: bfloat16 [2, 128, 4096], P(None, 'tile'), may hold values from 0 to 4
- beam_index: int32 [8, 2], P('beam'), may hold values from -16 to 16
- beam_weight: float32 [8], P('beam'), may hold values from 0.3 to 3
- probe_rows: int32 [256], P('tile'), may hold values from 0 to 16
- probe_cols: int32 [256], P('tile'), may hold values from 0 to 4095
Outputs:
- intensity: float32 [256, 256], P('tile', 'beam')
All inputs are finite; a program needn't handle non-finite values.
Results may differ from a plain program's by a relative error of at most 0.0003.
Values may be sent and summed in bfloat16 or wider, within the bound.
No kernel may reach another device: no remote copies, remote signals or barrier semaphores. Data moves between devices by JAX's collectives and lax.ppermute only.
A program may use at most 64 MiB of HBM per device.

v0:
```python
import math

import jax
import jax.numpy as jnp
from jax import lax
from jax.sharding import PartitionSpec as P

CROP = 16


def extended(block, sides, width):
    for axis, dim in sides:
        count = lax.axis_size(axis)
        forward = [(i, i + 1) for i in range(count - 1)]
        forward.append((count - 1, 0))
        backward = [(target, source) for source, target in forward]
        low = lax.ppermute(
            lax.slice_in_dim(block, block.shape[dim] - width, None, axis=dim), axis, forward
        )
        high = lax.ppermute(lax.slice_in_dim(block, 0, width, axis=dim), axis, backward)
        block = jnp.concatenate([low, block, high], axis=dim)
    return block


def make_taps():
    blur_raw = [math.exp(-((offset_index - 5) ** 2) / 4.5) for offset_index in range(11)]
    blur_total = sum(blur_raw)
    spread_raw = [math.exp(-((offset_index - 5) ** 2) / 18.0) for offset_index in range(11)]
    spread_total = sum(spread_raw)
    blur_list = [entry_value / blur_total for entry_value in blur_raw]
    cos_list = [
        spread_raw[offset_index] / spread_total * math.cos(0.35 * (offset_index - 5) ** 2)
        for offset_index in range(11)
    ]
    sin_list = [
        spread_raw[offset_index] / spread_total * math.sin(0.35 * (offset_index - 5) ** 2)
        for offset_index in range(11)
    ]
    return (blur_list, cos_list, sin_list)


def spread_columns(real_part, imag_part):
    blur_taps, cos_taps, sin_taps = make_taps()
    out_real = jnp.zeros_like(real_part)
    out_imag = jnp.zeros_like(imag_part)
    for offset_index in range(11):
        shift_real = jnp.roll(real_part, 5 - offset_index, axis=-1)
        shift_imag = jnp.roll(imag_part, 5 - offset_index, axis=-1)
        out_real = (
            out_real + cos_taps[offset_index] * shift_real - sin_taps[offset_index] * shift_imag
        )
        out_imag = (
            out_imag + cos_taps[offset_index] * shift_imag + sin_taps[offset_index] * shift_real
        )
    return (out_real, out_imag)


def spread_rows(padded_real, padded_imag):
    blur_taps, cos_taps, sin_taps = make_taps()
    out_rows = padded_real.shape[1] - 10
    out_real = jnp.zeros_like(padded_real[:, 0:out_rows])
    out_imag = jnp.zeros_like(padded_imag[:, 0:out_rows])
    for offset_index in range(11):
        shift_real = padded_real[:, offset_index : offset_index + out_rows]
        shift_imag = padded_imag[:, offset_index : offset_index + out_rows]
        out_real = (
            out_real + cos_taps[offset_index] * shift_real - sin_taps[offset_index] * shift_imag
        )
        out_imag = (
            out_imag + cos_taps[offset_index] * shift_imag + sin_taps[offset_index] * shift_real
        )
    return (out_real, out_imag)


def body(atom_counts, beam_index, beam_weight, probe_rows, probe_cols):
    blur_taps, cos_taps, sin_taps = make_taps()
    slice_count = atom_counts.shape[0]
    strip_rows = atom_counts.shape[1]
    grid_cols = atom_counts.shape[2]
    grid_rows = strip_rows * lax.axis_size("tile")
    first_row = lax.axis_index("tile") * strip_rows
    beam_total = beam_weight.shape[0] * lax.axis_size("beam")
    margin = 0
    padded_counts = extended(atom_counts, (("tile", 1),), 5)
    extent_rows = strip_rows + 2 * margin
    counts_float = padded_counts.astype(jnp.float32)
    along_rows = blur_taps[0] * counts_float[:, 0:extent_rows]
    for offset_index in range(1, 11):
        along_rows = (
            along_rows
            + blur_taps[offset_index] * counts_float[:, offset_index : offset_index + extent_rows]
        )
    blurred = blur_taps[0] * jnp.roll(along_rows, 5, axis=-1)
    for offset_index in range(1, 11):
        blurred = blurred + blur_taps[offset_index] * jnp.roll(
            along_rows, 5 - offset_index, axis=-1
        )
    local_rows = (first_row - margin + jnp.arange(extent_rows, dtype=jnp.int32)) % grid_rows
    col_grid = jnp.arange(grid_cols, dtype=jnp.int32)
    row_phase = (beam_index[:, 0:1] * local_rows[None, :] % grid_rows).astype(
        jnp.float32
    ) / grid_rows
    col_phase = (beam_index[:, 1:2] * col_grid[None, :] % grid_cols).astype(jnp.float32) / grid_cols
    angle_grid = 2.0 * math.pi * (row_phase[:, :, None] + col_phase[:, None, :])
    real_part = jnp.cos(angle_grid)
    imag_part = jnp.sin(angle_grid)
    for slice_index in range(slice_count):
        reach_rows = 0
        start_row = margin - reach_rows
        length_rows = strip_rows + 2 * reach_rows
        phase_now = 0.6 * blurred[slice_index, start_row : start_row + length_rows]
        cos_now = jnp.cos(phase_now)
        sin_now = jnp.sin(phase_now)
        real_part, imag_part = (
            real_part * cos_now - imag_part * sin_now,
            real_part * sin_now + imag_part * cos_now,
        )
        stacked = jnp.stack([real_part, imag_part])
        padded_wave = extended(stacked, (("tile", 2),), 5)
        padded_real, padded_imag = (padded_wave[0], padded_wave[1])
        real_part, imag_part = spread_rows(padded_real, padded_imag)
        real_part, imag_part = spread_columns(real_part, imag_part)
    probe_count = probe_rows.shape[0]
    crop_rows = probe_rows[:, None] + jnp.arange(CROP, dtype=jnp.int32)[None, :]
    crop_cols = (probe_cols[:, None] + jnp.arange(CROP, dtype=jnp.int32)[None, :]) % grid_cols
    crop_real = real_part[:, crop_rows[:, :, None], crop_cols[:, None, :]]
    crop_imag = imag_part[:, crop_rows[:, :, None], crop_cols[:, None, :]]
    global_rows = first_row + probe_rows
    probe_phase = (
        2.0
        * math.pi
        * (
            (beam_index[:, 0:1] * global_rows[None, :] % grid_rows).astype(jnp.float32) / grid_rows
            + (beam_index[:, 1:2] * probe_cols[None, :] % grid_cols).astype(jnp.float32) / grid_cols
        )
    )
    coef_real = beam_weight[:, None] * jnp.cos(probe_phase)
    coef_imag = -beam_weight[:, None] * jnp.sin(probe_phase)
    exit_real = jnp.einsum("bp,bpuv->puv", coef_real, crop_real) - jnp.einsum(
        "bp,bpuv->puv", coef_imag, crop_imag
    )
    exit_imag = jnp.einsum("bp,bpuv->puv", coef_real, crop_imag) + jnp.einsum(
        "bp,bpuv->puv", coef_imag, crop_real
    )
    terms = jnp.stack([exit_real, exit_imag], axis=1).reshape(probe_count, 2, CROP * CROP)
    summed = lax.psum_scatter(terms, "beam", scatter_dimension=2, tiled=True)
    return (summed[:, 0] * summed[:, 0] + summed[:, 1] * summed[:, 1]) / beam_total


def solution(mesh):
    return jax.shard_map(
        body,
        mesh=mesh,
        in_specs=(P(None, "tile", None), P("beam", None), P("beam"), P("tile"), P("tile")),
        out_specs=P("tile", "beam"),
        check_vma=False,
    )
```

profile of v0, /device:TPU:0, one launch (start us, length us, event | category | flops | bytes accessed | tf_op | source)
XLA Modules:
  0.0 396.5 jit_solution(12466964007497101715)
XLA Ops:
  6.5 1.1 fusion.107
  8.1 2.0 collective-permute-start.1
  10.2 1.3 fusion.108
  11.5 0.6 fusion.36
  12.0 0.8 fusion.28
  13.9 0.7 fusion.50
  14.8 1.2 fusion
  18.2 2.7 fusion.19
  20.9 3.8 subtract_bitcast_fusion.2
  24.7 0.7 collective-permute-start.2
  25.4 1.1 collective-permute-start.3
  26.5 1.8 cosine_multiply_fusion
  28.4 2.5 collective-permute-done.2
  30.8 2.3 collective-permute-done.3
  33.5 1.2 multiply_add_fusion.2
  34.7 1.2 multiply_subtract_fusion.2
  38.1 4.2 %subtract_bitcast_fusion.1 = (f32[1,1,32,4096]{3,2,1,0:T(8,128)S(1)}, f32[1,32,4096]{2,1,0:T(8,128)S(1)}, f32[1,32,4096]{2,1,0:T(8,128)S(1)}) fusion(f32[2,32,4096]{2,1,0:T(8,128)S(1)} %fusion.19, f32[1,32,5]{2,1,0:T(8,128)S(1)} %get-tuple-element.126, f32[1,32,4091]{2,1,0:T(8,128)S(1)} %get-tuple-element.128, f32[1,32,5]{2,1,0:T(8,128)S(1)} %get-tuple-element.81, ...), kind=kLoop, calls=%fused_computation.97 | loop fusion | flops 14417920 | bytes 13631488 | tf_op jit(solution)/shard_map/stack | solution.py:118
  42.2 2.0 add_bitcast_fusion.1
  44.4 2.3 collective-permute-start.5
  46.7 0.6 sine_multiply_fusion
  47.3 3.7 collective-permute-done.4
  51.0 1.9 collective-permute-done.5
  53.2 1.2 multiply_add_fusion
  55.4 1.2 multiply_subtract_fusion
  58.4 2.3 subtract_bitcast_fusion
  60.7 3.1 add_bitcast_fusion
  63.8 129.5 %gather_fusion = f32[16384]{0:T(1024)S(1)} fusion(f32[32,4096]{1,0:T(8,128)S(1)} %subtract_bitcast_fusion, s32[16384]{0:T(1024)S(1)} %reshape.2674), kind=kCustom, calls=%fused_computation | custom fusion | bytes 262144 | tf_op jit(solution)/shard_map/gather | solution.py:126
  193.5 0.9 copy.10
  194.4 129.5 %gather_fusion.1 = f32[16384]{0:T(1024)S(1)} fusion(f32[32,4096]{1,0:T(8,128)S(1)} %copy-done, s32[16384]{0:T(1024)S(1)} %reshape.2674), kind=kCustom, calls=%fused_computation.1 | custom fusion | bytes 262144 | tf_op jit(solution)/shard_map/gather | solution.py:127
  324.4 0.7 pad_maximum_fusion.46
  325.1 63.2 %reduce-scatter.2.cloned.1.call-done = f32[64,2,32]{0,2,1:T(8,128)} async-done(((f32[64,2,256]{0,2,1:T(8,128)}), f32[64,2,32]{0,2,1:T(8,128)}) %reduce-scatter.2.cloned.1.call-update) | async-done | bytes 16400 | tf_op jit(solution)/shard_map/reduce_scatter | solution.py:146
  388.3 1.3 fusion.39
  (73 shorter events, 9.7 us)
Async XLA Ops:
  6.5 8.0 %copy-start.1 = (bf16[2,32,4096]{2,1,0:T(8,128)(2,1)S(1)}, bf16[2,32,4096]{2,1,0:T(8,128)(2,1)}, u32[]{:S(2)}) copy-start(bf16[2,32,4096]{2,1,0:T(8,128)(2,1)} %param.5) | copy-start | bytes 1572868
  6.5 381.8 %reduce-scatter.2.cloned.1.call-start = ((), (), s32[]{:S(2)}) async-start(), calls=%async_computation.1 | async-start | bytes 294912 | tf_op jit(solution)/shard_map/reduce_scatter | solution.py:146
  7.6 7.0 %collective-permute-start = (bf16[2,5,4096]{2,1,0:T(8,128)(2,1)S(1)}, bf16[2,5,4096]{2,1,0:T(8,128)(2,1)S(1)}, u32[]{:S(2)}, u32[]{:S(2)}) collective-permute-start(bf16[2,5,4096]{2,1,0:T(8,128)(2,1)S(1)} %get-tuple-element.120), channel_id=1, source_target_pairs={{0,1},{1,2},{2,3},{3,0},{4,5},{5,6},{6,7},{7,4},{8,9},{9,10},{10,1... | collective-permute-start | bytes 245768 | tf_op jit(solution)/shard_map/ppermute | solution.py:17
  8.1 6.4 %collective-permute-start.1 = (bf16[2,5,4096]{2,1,0:T(8,128)(2,1)S(1)}, bf16[2,5,4096]{2,1,0:T(8,128)(2,1)S(1)}, u32[]{:S(2)}, u32[]{:S(2)}) collective-permute-start(bf16[2,5,4096]{2,1,0:T(8,128)(2,1)S(1)} %get-tuple-element.121), channel_id=1, source_target_pairs={{1,0},{2,1},{3,2},{0,3},{5,4},{6,5},{7,6},{4,7},{9,8},{10,9},{11,1... | collective-permute-start | bytes 245768 | tf_op jit(solution)/shard_map/ppermute | solution.py:20
  20.9 5.6 %copy-start.3 = (s32[64]{0:T(128)S(1)}, s32[64]{0:T(128)}, u32[]{:S(2)}) copy-start(s32[64]{0:T(128)} %param.8) | copy-start | bytes 772
  20.9 5.6 %copy-start.4 = (s32[64]{0:T(128)S(1)}, s32[64]{0:T(128)}, u32[]{:S(2)}) copy-start(s32[64]{0:T(128)} %param.9) | copy-start | bytes 772
  24.7 6.1 %collective-permute-start.2 = (f32[2,1,5,4096]{3,2,1,0:T(8,128)S(1)}, f32[2,1,5,4096]{3,2,1,0:T(8,128)S(1)}, u32[]{:S(2)}, u32[]{:S(2)}) collective-permute-start(f32[2,1,5,4096]{3,2,1,0:T(8,128)S(1)} %get-tuple-element.18), channel_id=1, source_target_pairs={{0,1},{1,2},{2,3},{3,0},{4,5},{5,6},{6,7},{7,4},{8,9},{9,10},{10,1... | collective-permute-start | bytes 491528 | tf_op jit(solution)/shard_map/ppermute | solution.py:17
  25.4 7.8 %collective-permute-start.3 = (f32[2,1,5,4096]{3,2,1,0:T(8,128)S(1)}, f32[2,1,5,4096]{3,2,1,0:T(8,128)S(1)}, u32[]{:S(2)}, u32[]{:S(2)}) collective-permute-start(f32[2,1,5,4096]{3,2,1,0:T(8,128)S(1)} %get-tuple-element.19), channel_id=1, source_target_pairs={{1,0},{2,1},{3,2},{0,3},{5,4},{6,5},{7,6},{4,7},{9,8},{10,9},{11,1... | collective-permute-start | bytes 491528 | tf_op jit(solution)/shard_map/ppermute | solution.py:20
  44.3 6.7 %collective-permute-start.4 = (f32[2,1,5,4096]{3,2,1,0:T(8,128)S(1)}, f32[2,1,5,4096]{3,2,1,0:T(8,128)S(1)}, u32[]{:S(2)}, u32[]{:S(2)}) collective-permute-start(f32[2,1,5,4096]{3,2,1,0:T(8,128)S(1)} %get-tuple-element.16), channel_id=1, source_target_pairs={{0,1},{1,2},{2,3},{3,0},{4,5},{5,6},{6,7},{7,4},{8,9},{9,10},{10,1... | collective-permute-start | bytes 491528 | tf_op jit(solution)/shard_map/ppermute | solution.py:17
  44.4 8.5 %collective-permute-start.5 = (f32[2,1,5,4096]{3,2,1,0:T(8,128)S(1)}, f32[2,1,5,4096]{3,2,1,0:T(8,128)S(1)}, u32[]{:S(2)}, u32[]{:S(2)}) collective-permute-start(f32[2,1,5,4096]{3,2,1,0:T(8,128)S(1)} %get-tuple-element.17), channel_id=1, source_target_pairs={{1,0},{2,1},{3,2},{0,3},{5,4},{6,5},{7,6},{4,7},{9,8},{10,9},{11,1... | collective-permute-start | bytes 491528 | tf_op jit(solution)/shard_map/ppermute | solution.py:20
  193.3 1.1 copy-start
  194.4 129.9 %copy-start.2 = (f32[64,16,16]{0,2,1:T(8,128)S(1)}, f32[64,16,16]{0,2,1:T(8,128)}, u32[]{:S(2)}) copy-start(f32[64,16,16]{0,2,1:T(8,128)} %copy.10) | copy-start | bytes 196612
  194.4 129.9 %copy-start.5 = (f32[64]{0:T(128)S(1)}, f32[64]{0:T(128)}, u32[]{:S(2)}) copy-start(f32[64]{0:T(128)} %get-tuple-element.5) | copy-start | bytes 772
  194.4 129.9 %copy-start.6 = (f32[64]{0:T(128)S(1)}, f32[64]{0:T(128)}, u32[]{:S(2)}) copy-start(f32[64]{0:T(128)} %sine_multiply_fusion) | copy-start | bytes 772
Sparse Core Ops, SparseCore 0:
  325.2 63.0 reduce-scatter.1
where the time goes:
time: 397 us
  local copies, waits for them, and re-layouts  270 us (68%)
  waiting for transfers between devices  73.6 us (19%)
  other arithmetic  31.5 us (8%)
  between operations  14.3 us (4%)
  starting transfers between devices  6.81 us (2%)
    gather x1, local copies, waits for them, and re-layouts, body(): crop_imag = imag_part[:, crop_rows[:, :, None], crop_cols[:, None, :]]  129 us
    gather x1, local copies, waits for them, and re-layouts, body(): crop_real = real_part[:, crop_rows[:, :, None], crop_cols[:, None, :]]  129 us
    reduce_scatter x1, waiting for transfers between devices, body(): summed = lax.psum_scatter(terms, 'beam', scatter_dimension=2, tiled=True)  63.2 us
    another operation x3, other arithmetic, body(): stacked = jnp.stack([real_part, imag_part])  9.9 us
  transfers between devices with their start and end apart: 7, of which 5 were waited for; matrix products, arithmetic and copies ran while one was open for 2% of the time, Pallas kernels for 0%

commit v1 on v0

v1 whole, which is shorter than its diff:
```python
import functools
import math

import jax
import jax.numpy as jnp
import numpy as np
from jax import lax
from jax.experimental import pallas as pl
from jax.experimental.pallas import tpu as pltpu
from jax.sharding import PartitionSpec as P

CROP = 16
REACH = 5
LANES = 128
HALF = 64
PAD = 16
PHASE = 0.6
MIDDLE = 1.2


def make_taps():
    blur = [math.exp(-(j * j) / 4.5) for j in range(-REACH, REACH + 1)]
    spread = [math.exp(-(j * j) / 18.0) for j in range(-REACH, REACH + 1)]
    blur = [value / sum(blur) for value in blur]
    spread = [value / sum(spread) for value in spread]
    angles = [0.35 * j * j for j in range(-REACH, REACH + 1)]
    real = [value * math.cos(angle) for value, angle in zip(spread, angles)]
    imag = [value * math.sin(angle) for value, angle in zip(spread, angles)]
    return blur, real, imag


def band(taps, shift=0):
    matrix = np.zeros((HALF, HALF))
    for column in range(HALF):
        for tap, value in enumerate(taps):
            if column + shift + tap < HALF:
                matrix[column + shift + tap, column] = value
    return matrix


def two_parts(matrix):
    high = np.asarray(matrix, np.float32).astype(jnp.bfloat16)
    low = (matrix - high.astype(np.float64)).astype(np.float32).astype(jnp.bfloat16)
    return high, low


def column_matrices():
    blur, real, imag = make_taps()
    real_band, imag_band = band(real), band(imag)
    blurs = []
    for shift in (0, REACH):
        blur_band = band(blur, shift)
        single = np.block([[blur_band, blur_band], [np.zeros((HALF, LANES))]])
        blurs.append(np.concatenate(two_parts(single), axis=0))
    blur_matrix = np.stack(blurs)
    spread = np.block(
        [
            [real_band, imag_band],
            [-imag_band, real_band],
            [-imag_band, real_band],
            [-real_band, -imag_band],
        ]
    )
    spread_high, spread_low = two_parts(spread)
    return blur_matrix, spread_high, spread_low


def fit(function, reach, degree):
    nodes = reach * np.cos(np.pi * (np.arange(200) + 0.5) / 200)
    series = np.polynomial.Chebyshev.fit(nodes, function(nodes), degree, domain=[-reach, reach])
    return series.convert(kind=np.polynomial.Polynomial).coef


def horner(coefficients, value):
    total = coefficients[-1]
    for coefficient in coefficients[-2::-1]:
        total = total * value + coefficient
    return total


def kernel(
    shape,
    rows_ref,
    cols_ref,
    origin_ref,
    main_ref,
    low_ref,
    high_ref,
    beam_ref,
    blur_ref,
    spread_high_ref,
    spread_low_ref,
    out_ref,
    strip,
    patch,
    smooth,
    start_wave,
    parts_high,
    parts_low,
    wave,
):
    grid_rows, grid_cols, beams, take_rows, take_cols = shape
    f32, bf16 = jnp.float32, jnp.bfloat16
    blur, real, imag = make_taps()
    tiles = grid_cols // LANES
    strip_rows = main_ref.shape[1]
    probes = out_ref.shape[0]
    octets = probes // 8
    span = strip_rows + 2 * PAD
    rows_first = take_rows + 6 * REACH
    rows_second = take_rows + 4 * REACH
    load_first = -(-rows_first // 8) * 8
    load_second = -(-rows_second // 8) * 8
    patch_rows = load_first + load_second
    first_row, first_col = origin_ref[0], origin_ref[1]

    def widen(tile, carry):
        lanes = pl.ds(pl.multiple_of(tile * LANES, LANES), LANES)
        for part in range(2):
            base = part * span
            strip[tile, base : base + PAD, :] = low_ref[part, :, lanes].astype(f32)
            strip[tile, base + PAD : base + PAD + strip_rows, :] = main_ref[part, :, lanes].astype(f32)
            strip[tile, base + PAD + strip_rows : base + span, :] = high_ref[part, :, lanes].astype(f32)
        return carry

    lax.fori_loop(0, tiles, widen, 0)

    lane = lax.broadcasted_iota(jnp.int32, (1, LANES), 1)

    def gather(probe, carry):
        row = rows_ref[probe] + first_row + (PAD - 3 * REACH)
        start = lax.rem(cols_ref[probe] + first_col + (grid_cols - 3 * REACH), grid_cols)
        tile = lax.div(start, LANES)
        offset = lax.rem(start, LANES)
        beside = lax.rem(tile + 1, tiles)
        shift = lax.rem(LANES - offset, LANES)
        keep = lane >= offset
        base = pl.multiple_of(probe * patch_rows, 8)
        for at, source, count in (
            (0, row, load_first),
            (load_first, row + span + REACH, load_second),
        ):
            here = strip[tile, pl.ds(source, count), :]
            there = strip[beside, pl.ds(source, count), :]
            moved = pltpu.roll(jnp.where(keep, here, there), shift, 1)
            patch[pl.ds(base + at, count), :] = moved
        return carry

    lax.fori_loop(0, probes, gather, 0, unroll=4)

    group = 8
    for part, source, target, count in (
        (0, 0, 0, rows_first),
        (1, load_first, rows_first, rows_second),
    ):
        for begin in range(0, count, group):
            chosen = range(begin, min(begin + group, count))
            stacked = jnp.concatenate(
                [
                    patch[pl.ds(source + r, probes, stride=patch_rows), :].astype(bf16)
                    for r in chosen
                ],
                axis=0,
            )
            result = jnp.dot(
                jnp.concatenate([stacked, stacked], axis=1),
                blur_ref[part],
                preferred_element_type=f32,
            )
            for at, r in enumerate(chosen):
                smooth[target + r] = result[at * probes : (at + 1) * probes]

    wave_rows = rows_second
    wave_tiles = -(-wave_rows // 8) * 8
    cos_turn = fit(lambda t: np.cos(2 * np.pi * np.sqrt(t + 0.125)), 0.125, 9)
    dx = (
        lax.broadcasted_iota(jnp.int32, (wave_tiles, LANES), 0) + (first_row - 2 * REACH)
    ).astype(f32) / grid_rows
    lanes_full = lax.broadcasted_iota(jnp.int32, (wave_tiles, LANES), 1)
    upper = lanes_full >= HALF
    dy = (
        jnp.where(upper, lanes_full - HALF, lanes_full) + (first_col - 2 * REACH)
    ).astype(f32) / grid_cols
    quarter = jnp.where(upper, 0.25, 0.0).astype(f32)

    def add_beam(beam, total):
        turns = beam_ref[beam, 0:1, :] * dx + beam_ref[beam, 1:2, :] * dy
        turns = turns - jnp.round(turns) - quarter
        turns = turns - jnp.round(turns)
        return total + beam_ref[beam, 2:3, :] * horner(
            [float(c) for c in cos_turn], turns * turns - 0.125
        )

    both = lax.fori_loop(0, beams, add_beam, jnp.zeros((wave_tiles, LANES), f32))
    swapped = pltpu.roll(both, HALF, 1)
    wave_real = jnp.where(upper, swapped, both)
    wave_imag = jnp.where(upper, both, -swapped)
    for r in range(wave_rows):
        start_wave[0, r] = jnp.broadcast_to(wave_real[r : r + 1], (8, LANES))
        start_wave[1, r] = jnp.broadcast_to(wave_imag[r : r + 1], (8, LANES))

    cos_fit = fit(lambda t: np.cos(t + MIDDLE), MIDDLE, 9)
    sin_fit = fit(lambda t: np.sin(t + MIDDLE), MIDDLE, 9)
    lane8 = lax.broadcasted_iota(jnp.int32, (8, LANES), 1)
    wave_fit = [
        jnp.where(lane8 < HALF, float(c), float(s)).astype(f32) for c, s in zip(cos_fit, sin_fit)
    ]
    sign8 = jnp.where(lane8 < HALF, -1.0, 1.0).astype(f32)

    def transmission(window):
        total = (PHASE * blur[REACH]) * window[REACH] - MIDDLE
        for j in range(1, REACH + 1):
            total = total + (PHASE * blur[REACH + j]) * (window[REACH - j] + window[REACH + j])
        return horner(wave_fit, total)

    def split_rows(window):
        real_sum = real[REACH] * window[REACH]
        imag_sum = None
        for j in range(1, REACH + 1):
            pair = window[REACH - j] + window[REACH + j]
            real_sum = real_sum + real[REACH + j] * pair
            term = imag[REACH + j] * pair
            imag_sum = term if imag_sum is None else imag_sum + term
        return real_sum, imag_sum

    def store_parts(slot, value, at, lanes):
        top = value.astype(bf16)
        parts_high[at, slot, lanes] = top.astype(f32)
        parts_low[at, slot, lanes] = value - top.astype(f32)

    def along_columns(count):
        top = parts_high[0:count].reshape(count * probes, 2 * LANES).astype(bf16)
        rest = parts_low[0:count].reshape(count * probes, 2 * LANES).astype(bf16)
        dot = functools.partial(jnp.dot, preferred_element_type=f32)
        return (
            dot(top, spread_high_ref[...])
            + dot(rest, spread_high_ref[...])
            + dot(top, spread_low_ref[...])
        )

    def first_slice(octet, carry):
        slot = pl.ds(pl.multiple_of(octet * 8, 8), 8)
        window, waves = [], []
        for r in range(rows_first):
            window.append(smooth[r, slot, :])
            if r < 2 * REACH:
                continue
            value = transmission(window)
            window.pop(0)
            at = r - 2 * REACH
            waves.append(start_wave[0, at] * value + start_wave[1, at] * pltpu.roll(value, HALF, 1))
            if at < 2 * REACH:
                continue
            real_sum, imag_sum = split_rows(waves)
            waves.pop(0)
            store_parts(slot, real_sum, at - 2 * REACH, slice(0, LANES))
            store_parts(slot, imag_sum, at - 2 * REACH, slice(LANES, 2 * LANES))
        return carry

    lax.fori_loop(0, octets, first_slice, 0)
    middle_rows = take_rows + 2 * REACH
    wave[...] = along_columns(middle_rows).reshape(middle_rows, probes, LANES)

    def second_slice(octet, carry):
        slot = pl.ds(pl.multiple_of(octet * 8, 8), 8)
        window, waves = [], []
        for r in range(rows_second):
            window.append(smooth[rows_first + r, slot, :])
            if r < 2 * REACH:
                continue
            value = transmission(window)
            window.pop(0)
            at = r - 2 * REACH
            now = wave[at, slot, :]
            turned = pltpu.roll(now, HALF, 1)
            now_real = jnp.where(lane8 < HALF, now, turned)
            now_imag = jnp.where(lane8 < HALF, turned, now) * sign8
            waves.append(now_real * value + now_imag * pltpu.roll(value, HALF, 1))
            if at < 2 * REACH:
                continue
            real_sum, imag_sum = split_rows(waves)
            waves.pop(0)
            store_parts(slot, real_sum, at - 2 * REACH, slice(0, LANES))
            store_parts(slot, imag_sum, at - 2 * REACH, slice(LANES, 2 * LANES))
        return carry

    lax.fori_loop(0, octets, second_slice, 0)
    final = along_columns(take_rows)
    power = final * final
    power = (power + pltpu.roll(power, HALF, 1)) * (1.0 / beams)
    lane_all = lax.broadcasted_iota(jnp.int32, (probes, LANES), 1)
    total = power[0:probes]
    for r in range(1, take_rows):
        moved = pltpu.roll(power[r * probes : (r + 1) * probes], r * take_cols, 1)
        total = jnp.where(lane_all >= r * take_cols, moved, total)
    out_ref[...] = total[:, 0 : take_rows * take_cols]


def body(atom_counts, beam_index, beam_weight, probe_rows, probe_cols):
    slices, strip_rows, grid_cols = atom_counts.shape
    beam_parts, tile_parts = lax.axis_size("beam"), lax.axis_size("tile")
    grid_rows = strip_rows * tile_parts
    beams = beam_weight.shape[0] * beam_parts
    probes = probe_rows.shape[0]
    pixels = CROP * CROP // beam_parts
    take_cols = min(pixels, CROP)
    take_rows = pixels // take_cols
    first_pixel = lax.axis_index("beam").astype(jnp.int32) * pixels
    origin = jnp.stack([first_pixel // CROP, first_pixel % CROP])

    forward = [(i, (i + 1) % tile_parts) for i in range(tile_parts)]
    backward = [(target, source) for source, target in forward]
    low = lax.ppermute(atom_counts[:, strip_rows - PAD :], "tile", forward)
    high = lax.ppermute(atom_counts[:, :PAD], "tile", backward)

    numbers = jnp.concatenate([beam_index.astype(jnp.float32), beam_weight[:, None]], axis=1)
    known = jnp.broadcast_to(
        jnp.pad(numbers, ((0, 0), (0, 5)))[:, :, None], (numbers.shape[0], 8, LANES)
    )
    reach = 1
    while reach < beam_parts:
        other = lax.ppermute(known, "beam", [(i, i ^ reach) for i in range(beam_parts)])
        known = jnp.concatenate([known, other], axis=0)
        reach *= 2

    blur_matrix, spread_high, spread_low = column_matrices()
    f32 = jnp.float32
    rows_first = take_rows + 6 * REACH
    rows_second = take_rows + 4 * REACH
    middle_rows = take_rows + 2 * REACH
    patch_rows = -(-rows_first // 8) * 8 + -(-rows_second // 8) * 8
    vmem = pl.BlockSpec(memory_space=pltpu.VMEM)
    smem = pl.BlockSpec(memory_space=pltpu.SMEM)
    call = pl.pallas_call(
        functools.partial(kernel, (grid_rows, grid_cols, beams, take_rows, take_cols)),
        out_shape=jax.ShapeDtypeStruct((probes, pixels), f32),
        in_specs=[smem] * 3 + [vmem] * 7,
        out_specs=vmem,
        scratch_shapes=[
            pltpu.VMEM((grid_cols // LANES, 2 * (strip_rows + 2 * PAD), LANES), f32),
            pltpu.VMEM((probes * patch_rows, LANES), f32),
            pltpu.VMEM((rows_first + rows_second, probes, LANES), f32),
            pltpu.VMEM((2, rows_second, 8, LANES), f32),
            pltpu.VMEM((middle_rows, probes, 2 * LANES), f32),
            pltpu.VMEM((middle_rows, probes, 2 * LANES), f32),
            pltpu.VMEM((middle_rows, probes, LANES), f32),
        ],
        name="window",
    )
    return call(
        probe_rows,
        probe_cols,
        origin,
        atom_counts,
        low,
        high,
        known,
        jnp.asarray(blur_matrix),
        jnp.asarray(spread_high),
        jnp.asarray(spread_low),
    )


def solution(mesh):
    return jax.shard_map(
        body,
        mesh=mesh,
        in_specs=(P(None, "tile", None), P("beam", None), P("beam"), P("tile"), P("tile")),
        out_specs=P("tile", "beam"),
        check_vma=False,
    )
```

time: 397 us -> 27.6 us (0.07)
  local copies, waits for them, and re-layouts: 270 us -> 3.34 us
  waiting for transfers between devices: 73.6 us -> 3.68 us
  other arithmetic: 31.5 us -> 1.28 us
  between operations: 14.3 us -> 0.7 us
  Pallas kernels: 0 us -> 8.67 us
    gather x2 -> x0, local copies, waits for them, and re-layouts: 259 us -> none  [the longest x1 129 us: body(): crop_imag = imag_part[:, crop_rows[:, :, None], crop_cols[:, None, :]]]
    reduce_scatter x1 -> x0, waiting for transfers between devices: 63.2 us -> none  [body(): summed = lax.psum_scatter(terms, 'beam', scatter_dimension=2, tiled=True)]
    another operation x4 -> x1, other arithmetic: 10.6 us -> 0.59 us  [body(): origin = jnp.stack([first_pixel // CROP, first_pixel % CROP])]
    add x5 -> x0, other arithmetic: 9.42 us -> none  [the longest x1 3.09 us: spread_columns(): out_imag + cos_taps[offset_index] * shift_imag]
    pallas_call x0 -> x1, Pallas kernels: none -> 8.67 us  [body(): call(probe_rows, probe_cols, origin, atom_counts, low, high, known, jnp.a...]
    slice x42 -> x1, local copies, waits for them, and re-layouts: 9.42 us -> 1.06 us  [body(): high = lax.ppermute(atom_counts[:, :PAD], 'tile', backward)]
    ppermute x6 -> x5, waiting for transfers between devices: 10.3 us -> 3.68 us  [the longest x3 3.04 us: body(): lax.ppermute(known, 'beam', [(i, i ^ reach) for i in range(beam_parts)])]
    sub x4 -> x0, other arithmetic: 4.79 us -> none  [the longest x2 2.43 us: spread_rows(): out_real + cos_taps[offset_index] * shift_real]
  transfers between devices with their start and end apart: 7 -> 5, of which waited for: 5 -> 3; matrix products, arithmetic and copies ran while one was open for 2% -> 8% of each run, Pallas kernels for 0% -> 0%
where the time goes in v1:
time: 27.6 us; the launch traced here: 27.1 us
  starting transfers between devices  9.46 us (34%)
  Pallas kernels  8.67 us (31%)
  waiting for transfers between devices  3.68 us (13%)
  local copies, waits for them, and re-layouts  3.34 us (12%)
  other arithmetic  1.28 us (5%)
  between operations  0.7 us (3%)
    pallas_call x1, Pallas kernels, body(): call(probe_rows, probe_cols, origin, atom_counts, low, high, known, jnp.a...  8.67 us
    ppermute x3, starting transfers between devices, body(): lax.ppermute(known, 'beam', [(i, i ^ reach) for i in range(beam_parts)])  7.66 us
    ppermute x3, waiting for transfers between devices, body(): lax.ppermute(known, 'beam', [(i, i ^ reach) for i in range(beam_parts)])  3.04 us
    ppermute x1, starting transfers between devices, body(): high = lax.ppermute(atom_counts[:, :PAD], 'tile', backward)  1.73 us
    pallas_call x1, local copies, waits for them, and re-layouts, body(): call(probe_rows, probe_cols, origin, atom_counts, low, high, known, jnp.a...  1.44 us
    slice x1, local copies, waits for them, and re-layouts, body(): high = lax.ppermute(atom_counts[:, :PAD], 'tile', backward)  1.06 us
    unnamed x6, local copies, waits for them, and re-layouts  0.77 us
    ppermute x1, waiting for transfers between devices, body(): high = lax.ppermute(atom_counts[:, :PAD], 'tile', backward)  0.64 us
  transfers between devices with their start and end apart: 5, of which 3 were waited for; matrix products, arithmetic and copies ran while one was open for 8% of the time, Pallas kernels for 0%

profile of v1, /device:TPU:0, one launch (start us, length us, event | category | flops | bytes accessed | tf_op | source)
XLA Modules:
  0.0 27.1 jit_solution(18188494254990679785)
XLA Ops:
  0.0 0.0 copy-start.2
  0.7 0.0 copy-done.2
  0.7 0.1 fusion.1
  0.8 0.1 broadcast_in_dim.13
  0.8 3.0 %collective-permute-start.2 = (f32[1,8,128]{2,1,0:T(8,128)S(1)}, f32[1,8,128]{2,1,0:T(8,128)S(1)}, u32[]{:S(2)}, u32[]{:S(2)}) collective-permute-start(f32[1,8,128]{2,1,0:T(8,128)S(1)} %broadcast_in_dim.13), channel_id=1, source_target_pairs={{0,4},{4,0},{8,12},{12,8},{16,20},{20,16},{24,28},{28,24},{1,5},{5... | collective-permute-start | bytes 12296 | tf_op jit(solution)/shard_map/ppermute | solution.py:322
  3.8 1.6 %collective-permute-done.2 = f32[1,8,128]{2,1,0:T(8,128)S(1)} collective-permute-done((f32[1,8,128]{2,1,0:T(8,128)S(1)}, f32[1,8,128]{2,1,0:T(8,128)S(1)}, u32[]{:S(2)}, u32[]{:S(2)}) %collective-permute-start.2) | collective-permute-done | bytes 4128 | tf_op jit(solution)/shard_map/ppermute | solution.py:322
  5.4 2.1 %collective-permute-start.3 = (f32[2,8,128]{2,1,0:T(8,128)S(1)}, f32[2,8,128]{2,1,0:T(8,128)S(1)}, u32[]{:S(2)}, u32[]{:S(2)}) collective-permute-start(f32[2,8,128]{2,1,0:T(8,128)S(1)} %pad_maximum_fusion.2), channel_id=1, source_target_pairs={{0,8},{4,12},{8,0},{12,4},{16,24},{20,28},{24,16},{28,20},{1,9},{5... | collective-permute-start | bytes 24584 | tf_op jit(solution)/shard_map/ppermute | solution.py:322
  7.5 1.1 %fusion.2 = (bf16[2,16,4096]{2,1,0:T(8,128)(2,1)S(1)}, bf16[2,16,4096]{2,1,0:T(8,128)(2,1)S(1)}) fusion(bf16[2,32,4096]{2,1,0:T(8,128)(2,1)} %main_ref.1), kind=kLoop, calls=%fused_computation.8 | loop fusion | bytes 1048576 | tf_op jit(solution)/shard_map/slice | solution.py:314
  8.6 0.1 collective-permute-start
  8.6 1.7 %collective-permute-start.1 = (bf16[2,16,4096]{2,1,0:T(8,128)(2,1)S(1)}, bf16[2,16,4096]{2,1,0:T(8,128)(2,1)S(1)}, u32[]{:S(2)}, u32[]{:S(2)}) collective-permute-start(bf16[2,16,4096]{2,1,0:T(8,128)(2,1)S(1)} %get-tuple-element.5), channel_id=1, source_target_pairs={{1,0},{2,1},{3,2},{0,3},{5,4},{6,5},{7,6},{4,7},{9,8},{10,9},{11,1... | collective-permute-start | bytes 786440 | tf_op jit(solution)/shard_map/ppermute | solution.py:314
  10.4 0.0 collective-permute-done.3
  10.4 2.6 %collective-permute-start.4 = (f32[4,8,128]{2,1,0:T(8,128)S(1)}, f32[4,8,128]{2,1,0:T(8,128)S(1)}, u32[]{:S(2)}, u32[]{:S(2)}) collective-permute-start(f32[4,8,128]{2,1,0:T(8,128)S(1)} %pad_maximum_fusion.1), channel_id=1, source_target_pairs={{0,16},{4,20},{8,24},{12,28},{16,0},{20,4},{24,8},{28,12},{1,17},{... | collective-permute-start | bytes 49160 | tf_op jit(solution)/shard_map/ppermute | solution.py:322
  13.0 0.6 %pad_add_fusion.origin_ref = s32[2]{0:T(128)} fusion(s32[1]{0:T(128)} %bitcast.1, s32[1]{0:T(128)} %bitcast), kind=kLoop, calls=%fused_computation.6 | loop fusion | flops 2 | bytes 16 | tf_op jit(solution)/shard_map/stack | solution.py:309
  13.6 1.5 %collective-permute-done.4 = f32[4,8,128]{2,1,0:T(8,128)S(1)} collective-permute-done((f32[4,8,128]{2,1,0:T(8,128)S(1)}, f32[4,8,128]{2,1,0:T(8,128)S(1)}, u32[]{:S(2)}, u32[]{:S(2)}) %collective-permute-start.4) | collective-permute-done | bytes 16416 | tf_op jit(solution)/shard_map/ppermute | solution.py:322
  15.0 0.6 %pad_maximum_fusion.beam_ref = f32[8,8,128]{2,1,0:T(8,128)} fusion(f32[4,8,128]{2,1,0:T(8,128)S(1)} %collective-permute-done.4, f32[2,8,128]{2,1,0:T(8,128)S(1)} %collective-permute-done.3, f32[1,8,128]{2,1,0:T(8,128)S(1)} %collective-permute-done.2, f32[1,8,128]{2,1,0:T(8,128)S(1)} %broadcast_in_dim.13), kind=kLoop, calls=%fused_computation | loop fusion | flops 24576 | bytes 65536 | tf_op jit(solution)/shard_map/concatenate | solution.py:323
  15.6 0.0 collective-permute-done.low_ref
  15.6 0.0 copy-start
  15.6 0.6 %collective-permute-done.1.high_ref = bf16[2,16,4096]{2,1,0:T(8,128)(2,1)S(1)} collective-permute-done((bf16[2,16,4096]{2,1,0:T(8,128)(2,1)S(1)}, bf16[2,16,4096]{2,1,0:T(8,128)(2,1)S(1)}, u32[]{:S(2)}, u32[]{:S(2)}) %collective-permute-start.1) | collective-permute-done | bytes 262176 | tf_op jit(solution)/shard_map/ppermute | solution.py:314
  16.3 0.1 copy-done
  16.3 0.0 copy-start.1
  16.3 0.7 %copy-done.1 = bf16[2,16,4096]{2,1,0:T(8,128)(2,1)} copy-done((bf16[2,16,4096]{2,1,0:T(8,128)(2,1)}, bf16[2,16,4096]{2,1,0:T(8,128)(2,1)S(1)}, u32[]{:S(2)}) %copy-start.1) | copy-done | bytes 262168
  17.0 8.7 %window.1 = f32[64,32]{1,0:T(8,128)} custom-call(s32[64]{0:T(128)} %rows_ref.1, s32[64]{0:T(128)} %cols_ref.1, s32[2]{0:T(128)} %pad_add_fusion.origin_ref, bf16[2,32,4096]{2,1,0:T(8,128)(2,1)} %main_ref.1, bf16[2,16,4096]{2,1,0:T(8,128)(2,1)} %copy-done, bf16[2,16,4096]{2,1,0:T(8,128)(2,1)} %copy-done.1, f32[8,8,128]{2,1,0:T(8,128)} %pad_maximum_fusion.beam_ref, ...), custom_call_target="tpu_custom_call" | custom-call | tf_op jit(solution)/shard_map/window/pallas_call | solution.py:350
  25.7 1.4 %copy.9 = f32[64,32]{0,1:T(8,128)} copy(f32[64,32]{1,0:T(8,128)} %window.1) | data formatting | bytes 16384 | tf_op jit(solution)/shard_map/window/pallas_call | solution.py:350
  (3 shorter events, 0.0 us)
Async XLA Ops:
  0.0 0.7 %copy-start.2 = (s32[1,2]{1,0:T(1,128)S(1)}, s32[1,2]{1,0:T(1,128)}, u32[]{:S(2)}) copy-start(s32[1,2]{1,0:T(1,128)} %param.9) | copy-start | bytes 28
  0.8 4.6 %collective-permute-start.2 = (f32[1,8,128]{2,1,0:T(8,128)S(1)}, f32[1,8,128]{2,1,0:T(8,128)S(1)}, u32[]{:S(2)}, u32[]{:S(2)}) collective-permute-start(f32[1,8,128]{2,1,0:T(8,128)S(1)} %broadcast_in_dim.13), channel_id=1, source_target_pairs={{0,4},{4,0},{8,12},{12,8},{16,20},{20,16},{24,28},{28,24},{1,5},{5... | collective-permute-start | bytes 12296 | tf_op jit(solution)/shard_map/ppermute | solution.py:322
  5.4 5.0 %collective-permute-start.3 = (f32[2,8,128]{2,1,0:T(8,128)S(1)}, f32[2,8,128]{2,1,0:T(8,128)S(1)}, u32[]{:S(2)}, u32[]{:S(2)}) collective-permute-start(f32[2,8,128]{2,1,0:T(8,128)S(1)} %pad_maximum_fusion.2), channel_id=1, source_target_pairs={{0,8},{4,12},{8,0},{12,4},{16,24},{20,28},{24,16},{28,20},{1,9},{5... | collective-permute-start | bytes 24584 | tf_op jit(solution)/shard_map/ppermute | solution.py:322
  8.6 7.1 %collective-permute-start = (bf16[2,16,4096]{2,1,0:T(8,128)(2,1)S(1)}, bf16[2,16,4096]{2,1,0:T(8,128)(2,1)S(1)}, u32[]{:S(2)}, u32[]{:S(2)}) collective-permute-start(bf16[2,16,4096]{2,1,0:T(8,128)(2,1)S(1)} %get-tuple-element.6), channel_id=1, source_target_pairs={{0,1},{1,2},{2,3},{3,0},{4,5},{5,6},{6,7},{7,4},{8,9},{9,10},{10,1... | collective-permute-start | bytes 786440 | tf_op jit(solution)/shard_map/ppermute | solution.py:313
  8.6 7.6 %collective-permute-start.1 = (bf16[2,16,4096]{2,1,0:T(8,128)(2,1)S(1)}, bf16[2,16,4096]{2,1,0:T(8,128)(2,1)S(1)}, u32[]{:S(2)}, u32[]{:S(2)}) collective-permute-start(bf16[2,16,4096]{2,1,0:T(8,128)(2,1)S(1)} %get-tuple-element.5), channel_id=1, source_target_pairs={{1,0},{2,1},{3,2},{0,3},{5,4},{6,5},{7,6},{4,7},{9,8},{10,9},{11,1... | collective-permute-start | bytes 786440 | tf_op jit(solution)/shard_map/ppermute | solution.py:314
  10.4 4.6 %collective-permute-start.4 = (f32[4,8,128]{2,1,0:T(8,128)S(1)}, f32[4,8,128]{2,1,0:T(8,128)S(1)}, u32[]{:S(2)}, u32[]{:S(2)}) collective-permute-start(f32[4,8,128]{2,1,0:T(8,128)S(1)} %pad_maximum_fusion.1), channel_id=1, source_target_pairs={{0,16},{4,20},{8,24},{12,28},{16,0},{20,4},{24,8},{28,12},{1,17},{... | collective-permute-start | bytes 49160 | tf_op jit(solution)/shard_map/ppermute | solution.py:322
  15.6 0.7 %copy-start = (bf16[2,16,4096]{2,1,0:T(8,128)(2,1)}, bf16[2,16,4096]{2,1,0:T(8,128)(2,1)S(1)}, u32[]{:S(2)}) copy-start(bf16[2,16,4096]{2,1,0:T(8,128)(2,1)S(1)} %collective-permute-done.low_ref) | copy-start | bytes 786436
  16.3 0.7 %copy-start.1 = (bf16[2,16,4096]{2,1,0:T(8,128)(2,1)}, bf16[2,16,4096]{2,1,0:T(8,128)(2,1)S(1)}, u32[]{:S(2)}) copy-start(bf16[2,16,4096]{2,1,0:T(8,128)(2,1)S(1)} %collective-permute-done.1.high_ref) | copy-start | bytes 786436

commit v2 on v0

v2 whole, which is shorter than its diff:
```python
import functools
import math

import jax
import jax.numpy as jnp
import numpy as np
from jax import lax
from jax.experimental import pallas as pl
from jax.experimental.pallas import tpu as pltpu
from jax.sharding import PartitionSpec as P


CROP = 16
REACH = 5
LANES = 128
HALF = 64
ROWS = 8
PAD = 16
PHASE = 0.6
MIDDLE = 1.2
NUMBERS = 3


def make_taps():
    blur = [math.exp(-(j * j) / 4.5) for j in range(-REACH, REACH + 1)]
    spread = [math.exp(-(j * j) / 18.0) for j in range(-REACH, REACH + 1)]
    blur = [value / sum(blur) for value in blur]
    spread = [value / sum(spread) for value in spread]
    angles = [0.35 * j * j for j in range(-REACH, REACH + 1)]
    real = [value * math.cos(angle) for value, angle in zip(spread, angles)]
    imag = [value * math.sin(angle) for value, angle in zip(spread, angles)]
    return np.array(blur), np.array(real), np.array(imag)


def two_parts(matrix):
    high = np.asarray(matrix, np.float32).astype(jnp.bfloat16)
    low = (matrix - high.astype(np.float64)).astype(np.float32).astype(jnp.bfloat16)
    return high, low


def band(taps, count):
    matrix = np.zeros((count, count + 2 * REACH))
    for i in range(count):
        matrix[i, i : i + 2 * REACH + 1] = taps
    return matrix


def row_blur(count, stored):
    taps = np.zeros((count, stored))
    taps[:, : count + 2 * REACH] = band(make_taps()[0], count)
    full = np.einsum("rk,pq->rpqk", taps, np.eye(ROWS)).reshape(count * ROWS, ROWS * stored)
    return np.concatenate(two_parts(full), axis=0)


def row_spread(count):
    _, real, imag = make_taps()
    real, imag = band(real, count), band(imag, count)
    taps = np.block([[real, -imag], [imag, real]])
    high, low = two_parts(np.kron(taps, np.eye(ROWS)))
    return np.concatenate([high, high, low], axis=1)


def column_band(taps):
    return np.kron(np.eye(2), np.pad(band(taps, HALF - 2 * REACH), ((0, 2 * REACH), (0, 0))).T)


def column_blur():
    high, low = two_parts(PHASE * column_band(make_taps()[0]))
    return np.block([[high, low], [high, np.zeros_like(low)]])


def column_spread():
    _, real, imag = make_taps()
    real, imag = column_band(real), column_band(imag)
    high, low = two_parts(np.block([[real, imag], [-imag, real]]))
    return np.concatenate([high, high, low], axis=0)


def fit(function, top, degree):
    nodes = top / 2 * (1 + np.cos(np.pi * (np.arange(200) + 0.5) / 200))
    series = np.polynomial.Chebyshev.fit(nodes, function(nodes), degree, domain=[0, top])
    return [float(c) for c in series.convert(kind=np.polynomial.Polynomial).coef]


def horner(coefficients, value):
    total = coefficients[-1]
    for coefficient in coefficients[-2::-1]:
        total = total * value + coefficient
    return total


def split(value):
    high = value.astype(jnp.bfloat16)
    return high, (value - high.astype(jnp.float32)).astype(jnp.bfloat16)


def product(left, right):
    return jnp.dot(left, right, preferred_element_type=jnp.float32)


def column_product(value, matrix):
    high, low = split(value)
    return product(jnp.concatenate([high, low, high], axis=1), matrix)


def row_product(matrix, value):
    high, low = split(value)
    return product(matrix, jnp.concatenate([high, low, high], axis=0))


def transmit(
    plan,
    part,
    rows_ref,
    cols_ref,
    main_ref,
    low_ref,
    high_ref,
    row_matrix,
    column_matrix,
    cos_out,
    sin_out,
    strip,
    patch,
):
    f32 = jnp.float32
    tiles = strip.shape[0]
    grid_cols = tiles * LANES
    strip_rows = main_ref.shape[1]
    halo = (3 - part) * REACH
    stored = patch.shape[0] * 2 // plan.probes
    first_row, first_col = plan.origin()

    def widen(tile, carry):
        lanes = pl.ds(pl.multiple_of(tile * LANES, LANES), LANES)
        strip[tile, 0:PAD, :] = low_ref[:, lanes].astype(f32)
        strip[tile, PAD : PAD + strip_rows, :] = main_ref[part, :, lanes].astype(f32)
        strip[tile, PAD + strip_rows :, :] = high_ref[:, lanes].astype(f32)
        return carry

    lax.fori_loop(0, tiles, widen, 0, unroll=4)
    lane = lax.broadcasted_iota(jnp.int32, (1, LANES), 1)

    def window(probe, place):
        row = rows_ref[probe] + (first_row + (PAD - halo))
        start = cols_ref[probe] + (first_col + (grid_cols - halo))
        start = jnp.where(start >= grid_cols, start - grid_cols, start)
        tile = lax.shift_right_logical(start, 7)
        offset = start & (LANES - 1)
        beside = jnp.where(tile == tiles - 1, 0, tile + 1)
        here = strip[tile, pl.ds(row, stored), :]
        there = strip[beside, pl.ds(row, stored), :]
        shift = (place + LANES - offset) & (LANES - 1)
        return pltpu.roll(jnp.where(lane >= offset, here, there), shift, 1)

    def gather(pair, carry):
        probe = lax.shift_right_logical(pair, 3) * (2 * ROWS) + (pair & (ROWS - 1))
        both = jnp.where(lane < HALF, window(probe, 0), window(probe + ROWS, HALF))
        at = pl.ds(pl.multiple_of(pair * stored, ROWS), stored)
        patch[at, :] = both.astype(patch.dtype)
        return carry

    lax.fori_loop(0, plan.probes // 2, gather, 0, unroll=8)

    cos_fit = fit(lambda t: np.cos(np.sqrt(t)), MIDDLE**2, 4)
    sin_fit = fit(lambda t: np.sinc(np.sqrt(t) / np.pi), MIDDLE**2, 4)
    count = ROWS * stored
    along = []
    for group in range(0, plan.groups, 2):
        counts = [patch[g * count : (g + 1) * count] for g in (group, group + 1)]
        counts = jnp.concatenate([value.astype(jnp.bfloat16) for value in counts], axis=1)
        both = product(row_matrix[...], counts)
        half = both.shape[0] // 2
        both = both[:half] + both[half:]
        along += [both[:, :LANES], both[:, LANES:]]
    phase = product(
        jnp.concatenate(split(jnp.concatenate(along, axis=0)), axis=1), column_matrix[...]
    )
    phase = phase[:, :LANES] + (phase[:, LANES:] - MIDDLE)
    square = phase * phase
    cos_out[...] = horner(cos_fit, square)
    sin_out[...] = phase * horner(sin_fit, square)


def common_wave(plan, beam_ref, wave_ref):
    f32 = jnp.float32
    count = wave_ref.shape[1] // ROWS
    shape = (-(-count // ROWS) * ROWS, LANES)
    beams = beam_ref[...]
    turn_fit = fit(lambda t: np.cos(2 * np.pi * np.sqrt(t)), 0.25, 9)
    first_row, first_col = plan.origin()
    dx = lax.broadcasted_iota(jnp.int32, shape, 0) + (first_row - 2 * REACH)
    lane = lax.broadcasted_iota(jnp.int32, shape, 1)
    upper = lane >= HALF
    dy = (lane & (HALF - 1)) + (first_col - 2 * REACH)
    dx = dx.astype(f32) * (1.0 / plan.grid_rows)
    dy = dy.astype(f32) * (1.0 / plan.grid_cols)
    quarter = jnp.where(upper, 0.25, 0.0).astype(f32)

    both = jnp.zeros(shape, f32)
    for beam in range(plan.beams):
        row, col, weight = [beams[beam : beam + 1, i : i + 1] for i in range(NUMBERS)]
        turns = row * dx + col * dy
        turns = turns - jnp.round(turns) - quarter
        turns = turns - jnp.round(turns)
        both = both + weight * horner(turn_fit, turns * turns)
    turned = pltpu.roll(both, HALF, 1)
    real = jnp.where(upper, turned, both)
    imag = jnp.where(upper, both, turned)
    for r in range(count):
        at = slice(r * ROWS, (r + 1) * ROWS)
        wave_ref[0, at, :] = jnp.broadcast_to(real[r : r + 1], (ROWS, LANES))
        wave_ref[1, at, :] = jnp.broadcast_to(imag[r : r + 1], (ROWS, LANES))


def propagate(waves, row_matrix, column_matrix):
    rows = []
    for i in range(0, len(waves), 2):
        both = row_product(row_matrix[...], jnp.concatenate(waves[i : i + 2], axis=1))
        half = both.shape[0] // 2
        for lanes in (slice(0, LANES), slice(LANES, 2 * LANES)):
            rows.append(jnp.concatenate([both[:half, lanes], both[half:, lanes]], axis=1))
    return column_product(jnp.concatenate(rows, axis=0), column_matrix[...])


def turn(real, imag, cos, sin):
    return jnp.concatenate([real * cos - imag * sin, real * sin + imag * cos], axis=0)


class Plan:
    def __init__(self, grid_rows, grid_cols, beams, probes, pixels):
        self.grid_rows, self.grid_cols = grid_rows, grid_cols
        self.beams, self.probes, self.pixels = beams, probes, pixels
        self.groups = probes // (2 * ROWS)
        self.take_cols = min(pixels, CROP)
        self.take_rows = pixels // self.take_cols
        self.phase_rows = [self.take_rows + 4 * REACH, self.take_rows + 2 * REACH]
        self.stored = [-(-(count + 2 * REACH) // ROWS) * ROWS for count in self.phase_rows]

    def origin(self):
        first = lax.axis_index("beam").astype(jnp.int32) * self.pixels
        return first // CROP, first % CROP


def finish(
    plan,
    beam_ref,
    cos_0,
    sin_0,
    cos_1,
    sin_1,
    spread_rows_0,
    spread_rows_1,
    spread_cols,
    out_ref,
    start,
):
    common_wave(plan, beam_ref, start)
    count = plan.phase_rows[0] * ROWS
    waves = []
    for group in range(plan.groups):
        at = slice(group * count, (group + 1) * count)
        waves.append(turn(start[0], start[1], cos_0[at], sin_0[at]))
    wave = propagate(waves, spread_rows_0, spread_cols)
    count = plan.phase_rows[1] * ROWS
    waves = []
    for group in range(plan.groups):
        at = slice(group * count, (group + 1) * count)
        waves.append(turn(wave[at, :LANES], wave[at, LANES:], cos_1[at], sin_1[at]))
    wave = propagate(waves, spread_rows_1, spread_cols)
    lane = lax.broadcasted_iota(jnp.int32, (ROWS, LANES), 1)
    blocks = []
    count = plan.take_rows * ROWS
    for group in range(plan.groups):
        final = wave[group * count : (group + 1) * count]
        real, imag = final[:, :LANES], final[:, LANES:]
        power = (real * real + imag * imag) * (1.0 / plan.beams)
        for place in (0, HALF):
            block = None
            for r in range(plan.take_rows):
                moved = power[r * ROWS : (r + 1) * ROWS]
                shift = (r * plan.take_cols - place) % LANES
                moved = pltpu.roll(moved, shift, 1) if shift else moved
                block = moved if r == 0 else jnp.where(lane < r * plan.take_cols, block, moved)
            blocks.append(block)
    out_ref[...] = jnp.concatenate(blocks, axis=0).T[: plan.pixels]


def window(atom_counts, beam_index, beam_weight, probe_rows, probe_cols):
    _, strip_rows, grid_cols = atom_counts.shape
    beam_parts, tile_parts = lax.axis_size("beam"), lax.axis_size("tile")
    plan = Plan(
        strip_rows * tile_parts,
        grid_cols,
        beam_weight.shape[0] * beam_parts,
        probe_rows.shape[0],
        CROP * CROP // beam_parts,
    )

    forward = [(i, (i + 1) % tile_parts) for i in range(tile_parts)]
    backward = [(target, source) for source, target in forward]
    known = jnp.concatenate([beam_index.astype(jnp.float32), beam_weight[:, None]], axis=1)
    known = jnp.pad(known, ((0, 0), (0, LANES - NUMBERS)))
    edges = [
        (atom_counts[part, strip_rows - PAD :], atom_counts[part, :PAD]) for part in range(2)
    ]
    known, edges = lax.optimization_barrier((known, edges))

    def share(known, reach):
        other = lax.ppermute(known, "beam", [(i, i ^ reach) for i in range(beam_parts)])
        return jnp.concatenate([known, other], axis=0)

    halos = []
    for part in range(2):
        low = lax.ppermute(edges[part][0], "tile", forward)
        high = lax.ppermute(edges[part][1], "tile", backward)
        halos.append((low, high))
    reach = 1
    while reach < beam_parts:
        known = share(known, reach)
        reach *= 2

    f32, bf16 = jnp.float32, jnp.bfloat16
    vmem = pl.BlockSpec(memory_space=pltpu.VMEM)
    smem = pl.BlockSpec(memory_space=pltpu.SMEM)
    phases = [(plan.groups * count * ROWS, LANES) for count in plan.phase_rows]
    columns = jnp.asarray(column_blur())

    def phase_call(part):
        stored = plan.stored[part]
        low, high = halos[part]
        shape = jax.ShapeDtypeStruct(phases[part], f32)
        kind = bf16 if stored % (2 * ROWS) == 0 else f32
        call = pl.pallas_call(
            functools.partial(transmit, plan, part),
            out_shape=[shape, shape],
            in_specs=[smem] * 2 + [vmem] * 5,
            out_specs=[vmem] * 2,
            scratch_shapes=[
                pltpu.VMEM((grid_cols // LANES, strip_rows + 2 * PAD, LANES), f32),
                pltpu.VMEM((plan.probes // 2 * stored, LANES), kind),
            ],
            compiler_params=pltpu.CompilerParams(vmem_limit_bytes=12 << 20),
        )
        matrix = jnp.asarray(row_blur(plan.phase_rows[part], stored))
        return call(probe_rows, probe_cols, atom_counts, low, high, matrix, columns)

    cos_1, sin_1 = phase_call(1)
    cos_0, sin_0 = phase_call(0)
    call = pl.pallas_call(
        functools.partial(finish, plan),
        out_shape=jax.ShapeDtypeStruct((plan.pixels, plan.probes), f32),
        in_specs=[vmem] * 8,
        out_specs=vmem,
        scratch_shapes=[pltpu.VMEM((2, plan.phase_rows[0] * ROWS, LANES), f32)],
        compiler_params=pltpu.CompilerParams(vmem_limit_bytes=12 << 20),
        name="finish",
    )
    matrices = [
        row_spread(plan.phase_rows[1]),
        row_spread(plan.take_rows),
        column_spread(),
    ]
    out = call(known, cos_0, sin_0, cos_1, sin_1, *[jnp.asarray(m) for m in matrices])
    return out.T


def solution(mesh):
    return jax.shard_map(
        window,
        mesh=mesh,
        in_specs=(P(None, "tile", None), P("beam", None), P("beam"), P("tile"), P("tile")),
        out_specs=P("tile", "beam"),
        check_vma=False,
    )
```

time: 397 us -> 23.3 us (0.06)
  local copies, waits for them, and re-layouts: 270 us -> 1.26 us
  waiting for transfers between devices: 73.6 us -> 3.46 us
  other arithmetic: 31.5 us -> 0.11 us
  between operations: 14.3 us -> 0.88 us
  Pallas kernels: 0 us -> 6.05 us
  starting transfers between devices: 6.81 us -> 11.2 us
    gather x2 -> x0, local copies, waits for them, and re-layouts: 259 us -> none  [the longest x1 129 us: body(): crop_imag = imag_part[:, crop_rows[:, :, None], crop_cols[:, None, :]]]
    reduce_scatter x1 -> x0, waiting for transfers between devices: 63.2 us -> none  [body(): summed = lax.psum_scatter(terms, 'beam', scatter_dimension=2, tiled=True)]
    another operation x4 -> x0, other arithmetic: 10.6 us -> none  [the longest x3 9.9 us: body(): stacked = jnp.stack([real_part, imag_part])]
    slice x42 -> x0, local copies, waits for them, and re-layouts: 9.42 us -> none  [the longest x20 3.53 us: spread_columns(): shift_real = jnp.roll(real_part, 5 - offset_index, axis=-1)]
    add x5 -> x0, other arithmetic: 9.42 us -> none  [the longest x1 3.09 us: spread_columns(): out_imag + cos_taps[offset_index] * shift_imag]
    ppermute x6 -> x7, waiting for transfers between devices: 10.3 us -> 3.46 us  [the longest x3 3.45 us: share(): lax.ppermute(known, 'beam', [(i, i ^ reach) for i in range(beam_parts)])]
    pallas_call x0 -> x3, Pallas kernels: none -> 6.05 us  [the longest x2 3.8 us: phase_call(): return call(probe_rows, probe_cols, atom_counts, low, high, matrix, columns)]
    sub x4 -> x0, other arithmetic: 4.79 us -> none  [the longest x2 2.43 us: spread_rows(): out_real + cos_taps[offset_index] * shift_real]
  transfers between devices with their start and end apart: 7 -> 7, of which waited for: 5 -> 2; matrix products, arithmetic and copies ran while one was open for 2% -> 0% of each run, Pallas kernels for 0% -> 8%
where the time goes in v2:
time: 23.3 us; the launch traced here: 23 us
  starting transfers between devices  11.2 us (48%)
  Pallas kernels  6.05 us (26%)
  waiting for transfers between devices  3.46 us (15%)
  local copies, waits for them, and re-layouts  1.26 us (5%)
  between operations  0.88 us (4%)
    ppermute x3, starting transfers between devices, share(): lax.ppermute(known, 'beam', [(i, i ^ reach) for i in range(beam_parts)])  7.73 us
    pallas_call x2, Pallas kernels, phase_call(): return call(probe_rows, probe_cols, atom_counts, low, high, matrix, columns)  3.8 us
    ppermute x2, starting transfers between devices, window(): high = lax.ppermute(edges[part][1], 'tile', backward)  3.49 us
    ppermute x3, waiting for transfers between devices, share(): lax.ppermute(known, 'beam', [(i, i ^ reach) for i in range(beam_parts)])  3.45 us
    pallas_call x1, Pallas kernels, window(): call(known, cos_0, sin_0, cos_1, sin_1, *[jnp.asarray(m) for m in matrices])  2.25 us
    squeeze x1, local copies, waits for them, and re-layouts, window(): atom_counts[part, :PAD]  1.2 us
  transfers between devices with their start and end apart: 7, of which 2 were waited for; matrix products, arithmetic and copies ran while one was open for 0% of the time, Pallas kernels for 8%

profile of v2, /device:TPU:0, one launch (start us, length us, event | category | flops | bytes accessed | tf_op | source)
XLA Modules:
  0.0 23.0 jit_solution(17666322674758858095)
XLA Ops:
  0.7 0.0 copy-done.9
  0.7 0.0 copy-start
  0.7 0.0 copy-start.1
  0.7 0.0 copy-start.5
  0.7 1.2 %slice_bitcast_fusion = (bf16[16,4096]{1,0:T(8,128)(2,1)S(1)}, bf16[16,4096]{1,0:T(8,128)(2,1)S(1)}, bf16[16,4096]{1,0:T(8,128)(2,1)S(1)}, bf16[16,4096]{1,0:T(8,128)(2,1)S(1)}) fusion(bf16[2,32,4096]{2,1,0:T(8,128)(2,1)} %main_ref.3), kind=kLoop, calls=%fused_computation | loop fusion | bytes 1048576 | tf_op jit(solution)/shard_map/squeeze | solution.py:305
  1.9 0.1 fusion
  2.0 3.0 %collective-permute-start = (f32[1,128]{1,0:T(1,128)S(1)}, f32[1,128]{1,0:T(1,128)S(1)}, u32[]{:S(2)}, u32[]{:S(2)}) collective-permute-start(f32[1,128]{1,0:T(1,128)S(1)} %fusion), channel_id=1, source_target_pairs={{0,4},{4,0},{8,12},{12,8},{16,20},{20,16},{24,28},{28,24},{1,5},{5... | collective-permute-start | bytes 1544 | tf_op jit(solution)/shard_map/ppermute | solution.py:310
  5.0 1.5 %collective-permute-done = f32[1,128]{1,0:T(1,128)S(1)} collective-permute-done((f32[1,128]{1,0:T(1,128)S(1)}, f32[1,128]{1,0:T(1,128)S(1)}, u32[]{:S(2)}, u32[]{:S(2)}) %collective-permute-start) | collective-permute-done | bytes 544 | tf_op jit(solution)/shard_map/ppermute | solution.py:310
  6.5 2.1 %collective-permute-start.1 = (f32[2,128]{1,0:T(2,128)S(1)}, f32[2,128]{1,0:T(2,128)S(1)}, u32[]{:S(2)}, u32[]{:S(2)}) collective-permute-start(f32[2,128]{1,0:T(2,128)S(1)} %pad_maximum_fusion.2), channel_id=1, source_target_pairs={{0,8},{4,12},{8,0},{12,4},{16,24},{20,28},{24,16},{28,20},{1,9},{5... | collective-permute-start | bytes 3080 | tf_op jit(solution)/shard_map/ppermute | solution.py:310
  8.6 0.0 collective-permute-start.3
  8.6 1.7 %collective-permute-start.4 = (bf16[16,4096]{1,0:T(8,128)(2,1)S(1)}, bf16[16,4096]{1,0:T(8,128)(2,1)S(1)}, u32[]{:S(2)}, u32[]{:S(2)}) collective-permute-start(bf16[16,4096]{1,0:T(8,128)(2,1)S(1)} %get-tuple-element.16), channel_id=1, source_target_pairs={{1,0},{2,1},{3,2},{0,3},{5,4},{6,5},{7,6},{4,7},{9,8},{10,9},{11,1... | collective-permute-start | bytes 393224 | tf_op jit(solution)/shard_map/ppermute | solution.py:316
  10.4 0.0 collective-permute-start.5
  10.4 1.7 %collective-permute-start.6 = (bf16[16,4096]{1,0:T(8,128)(2,1)S(1)}, bf16[16,4096]{1,0:T(8,128)(2,1)S(1)}, u32[]{:S(2)}, u32[]{:S(2)}) collective-permute-start(bf16[16,4096]{1,0:T(8,128)(2,1)S(1)} %get-tuple-element.20), channel_id=1, source_target_pairs={{1,0},{2,1},{3,2},{0,3},{5,4},{6,5},{7,6},{4,7},{9,8},{10,9},{11,1... | collective-permute-start | bytes 393224 | tf_op jit(solution)/shard_map/ppermute | solution.py:316
  12.1 0.0 collective-permute-done.1
  12.1 0.0 copy-start.7
  12.2 0.0 copy-start.8
  12.2 2.7 %collective-permute-start.2 = (f32[4,128]{1,0:T(4,128)S(1)}, f32[4,128]{1,0:T(4,128)S(1)}, u32[]{:S(2)}, u32[]{:S(2)}) collective-permute-start(f32[4,128]{1,0:T(4,128)S(1)} %pad_maximum_fusion.1), channel_id=1, source_target_pairs={{0,16},{4,20},{8,24},{12,28},{16,0},{20,4},{24,8},{28,12},{1,17},{... | collective-permute-start | bytes 6152 | tf_op jit(solution)/shard_map/ppermute | solution.py:310
  14.8 1.9 %collective-permute-done.2 = f32[4,128]{1,0:T(4,128)S(1)} collective-permute-done((f32[4,128]{1,0:T(4,128)S(1)}, f32[4,128]{1,0:T(4,128)S(1)}, u32[]{:S(2)}, u32[]{:S(2)}) %collective-permute-start.2) | collective-permute-done | bytes 2080 | tf_op jit(solution)/shard_map/ppermute | solution.py:310
  16.7 0.0 copy-start.4
  16.7 0.0 collective-permute-done.5.low_ref
  16.8 0.0 collective-permute-done.6.high_ref
  16.8 0.0 copy-done
  16.8 0.0 copy-done.1
  16.8 0.0 copy-done.5
  16.8 1.8 %shard_map.110 = (f32[384,128]{1,0:T(8,128)S(1)}, f32[384,128]{1,0:T(8,128)S(1)}) custom-call(s32[64]{0:T(128)S(1)} %copy-done.7, s32[64]{0:T(128)S(1)} %copy-done.8, bf16[2,32,4096]{2,1,0:T(8,128)(2,1)S(1)} %copy-done, bf16[16,4096]{1,0:T(8,128)(2,1)S(1)} %collective-permute-done.5.low_ref, bf16[16,4096]{1,0:T(8,128)(2,1)S(1)} %collective-permute-done.6.high_ref, ...), custom_call_target="tpu_custom_call" | custom-call | tf_op jit(solution)/shard_map/pallas_call | solution.py:346
  18.7 0.0 copy-start.2
  18.7 0.0 copy-start.3
  18.7 0.0 copy-start.6
  18.7 0.0 collective-permute-done.3.low_ref
  18.7 0.0 collective-permute-done.4.high_ref
  18.7 2.0 %shard_map.109 = (f32[704,128]{1,0:T(8,128)S(1)}, f32[704,128]{1,0:T(8,128)S(1)}) custom-call(s32[64]{0:T(128)S(1)} %copy-done.7, s32[64]{0:T(128)S(1)} %copy-done.8, bf16[2,32,4096]{2,1,0:T(8,128)(2,1)S(1)} %copy-done, bf16[16,4096]{1,0:T(8,128)(2,1)S(1)} %collective-permute-done.3.low_ref, bf16[16,4096]{1,0:T(8,128)(2,1)S(1)} %collective-permute-done.4.high_ref, ...), custom_call_target="tpu_custom_call" | custom-call | tf_op jit(solution)/shard_map/pallas_call | solution.py:346
  20.7 2.3 %finish.1 = f32[32,64]{1,0:T(8,128)} custom-call(f32[8,128]{1,0:T(8,128)S(1)} %pad_maximum_fusion.beam_ref, f32[704,128]{1,0:T(8,128)S(1)} %get-tuple-element.17.cos_0, f32[704,128]{1,0:T(8,128)S(1)} %get-tuple-element.18.sin_0, f32[384,128]{1,0:T(8,128)S(1)} %get-tuple-element.21.cos_1, f32[384,128]{1,0:T(8,128)S(1)} %get-tuple-element.22.sin_1, ...), custom_call_target="tpu_custom_call" | custom-call | tf_op jit(solution)/shard_map/finish/pallas_call | solution.py:364
  (11 shorter events, 0.0 us)
Async XLA Ops:
  0.0 0.7 %copy-start.9 = (s32[1,2]{1,0:T(1,128)S(1)}, s32[1,2]{1,0:T(1,128)}, u32[]{:S(2)}) copy-start(s32[1,2]{1,0:T(1,128)} %param.12) | copy-start | bytes 28
  0.7 16.1 %copy-start = (bf16[2,32,4096]{2,1,0:T(8,128)(2,1)S(1)}, bf16[2,32,4096]{2,1,0:T(8,128)(2,1)}, u32[]{:S(2)}) copy-start(bf16[2,32,4096]{2,1,0:T(8,128)(2,1)} %main_ref.3) | copy-start | bytes 1572868
  0.7 16.1 %copy-start.1 = (bf16[256,256]{1,0:T(8,128)(2,1)S(1)}, bf16[256,256]{1,0:T(8,128)(2,1)}, u32[]{:S(2)}) copy-start(bf16[256,256]{1,0:T(8,128)(2,1)} %constant.15.clone.column_matrix) | copy-start | bytes 393220
  0.7 16.1 %copy-start.5 = (bf16[192,192]{1,0:T(8,128)(2,1)S(1)}, bf16[192,192]{1,0:T(8,128)(2,1)}, u32[]{:S(2)}) copy-start(bf16[192,192]{1,0:T(8,128)(2,1)} %constant.16.clone.row_matrix) | copy-start | bytes 221188
  2.0 4.5 %collective-permute-start = (f32[1,128]{1,0:T(1,128)S(1)}, f32[1,128]{1,0:T(1,128)S(1)}, u32[]{:S(2)}, u32[]{:S(2)}) collective-permute-start(f32[1,128]{1,0:T(1,128)S(1)} %fusion), channel_id=1, source_target_pairs={{0,4},{4,0},{8,12},{12,8},{16,20},{20,16},{24,28},{28,24},{1,5},{5... | collective-permute-start | bytes 1544 | tf_op jit(solution)/shard_map/ppermute | solution.py:310
  6.5 5.6 %collective-permute-start.1 = (f32[2,128]{1,0:T(2,128)S(1)}, f32[2,128]{1,0:T(2,128)S(1)}, u32[]{:S(2)}, u32[]{:S(2)}) collective-permute-start(f32[2,128]{1,0:T(2,128)S(1)} %pad_maximum_fusion.2), channel_id=1, source_target_pairs={{0,8},{4,12},{8,0},{12,4},{16,24},{20,28},{24,16},{28,20},{1,9},{5... | collective-permute-start | bytes 3080 | tf_op jit(solution)/shard_map/ppermute | solution.py:310
  8.6 10.1 %collective-permute-start.3 = (bf16[16,4096]{1,0:T(8,128)(2,1)S(1)}, bf16[16,4096]{1,0:T(8,128)(2,1)S(1)}, u32[]{:S(2)}, u32[]{:S(2)}) collective-permute-start(bf16[16,4096]{1,0:T(8,128)(2,1)S(1)} %get-tuple-element.15), channel_id=1, source_target_pairs={{0,1},{1,2},{2,3},{3,0},{4,5},{5,6},{6,7},{7,4},{8,9},{9,10},{10,1... | collective-permute-start | bytes 393224 | tf_op jit(solution)/shard_map/ppermute | solution.py:315
  8.6 10.1 %collective-permute-start.4 = (bf16[16,4096]{1,0:T(8,128)(2,1)S(1)}, bf16[16,4096]{1,0:T(8,128)(2,1)S(1)}, u32[]{:S(2)}, u32[]{:S(2)}) collective-permute-start(bf16[16,4096]{1,0:T(8,128)(2,1)S(1)} %get-tuple-element.16), channel_id=1, source_target_pairs={{1,0},{2,1},{3,2},{0,3},{5,4},{6,5},{7,6},{4,7},{9,8},{10,9},{11,1... | collective-permute-start | bytes 393224 | tf_op jit(solution)/shard_map/ppermute | solution.py:316
  10.4 6.4 %collective-permute-start.5 = (bf16[16,4096]{1,0:T(8,128)(2,1)S(1)}, bf16[16,4096]{1,0:T(8,128)(2,1)S(1)}, u32[]{:S(2)}, u32[]{:S(2)}) collective-permute-start(bf16[16,4096]{1,0:T(8,128)(2,1)S(1)} %get-tuple-element.19), channel_id=1, source_target_pairs={{0,1},{1,2},{2,3},{3,0},{4,5},{5,6},{6,7},{7,4},{8,9},{9,10},{10,1... | collective-permute-start | bytes 393224 | tf_op jit(solution)/shard_map/ppermute | solution.py:315
  10.4 6.4 %collective-permute-start.6 = (bf16[16,4096]{1,0:T(8,128)(2,1)S(1)}, bf16[16,4096]{1,0:T(8,128)(2,1)S(1)}, u32[]{:S(2)}, u32[]{:S(2)}) collective-permute-start(bf16[16,4096]{1,0:T(8,128)(2,1)S(1)} %get-tuple-element.20), channel_id=1, source_target_pairs={{1,0},{2,1},{3,2},{0,3},{5,4},{6,5},{7,6},{4,7},{9,8},{10,9},{11,1... | collective-permute-start | bytes 393224 | tf_op jit(solution)/shard_map/ppermute | solution.py:316
  12.1 4.7 %copy-start.7 = (s32[64]{0:T(128)S(1)}, s32[64]{0:T(128)}, u32[]{:S(2)}) copy-start(s32[64]{0:T(128)} %rows_ref.3) | copy-start | bytes 772
  12.2 4.6 %copy-start.8 = (s32[64]{0:T(128)S(1)}, s32[64]{0:T(128)}, u32[]{:S(2)}) copy-start(s32[64]{0:T(128)} %cols_ref.3) | copy-start | bytes 772
  12.2 4.5 %collective-permute-start.2 = (f32[4,128]{1,0:T(4,128)S(1)}, f32[4,128]{1,0:T(4,128)S(1)}, u32[]{:S(2)}, u32[]{:S(2)}) collective-permute-start(f32[4,128]{1,0:T(4,128)S(1)} %pad_maximum_fusion.1), channel_id=1, source_target_pairs={{0,16},{4,20},{8,24},{12,28},{16,0},{20,4},{24,8},{28,12},{1,17},{... | collective-permute-start | bytes 6152 | tf_op jit(solution)/shard_map/ppermute | solution.py:310
  16.7 2.0 %copy-start.4 = (bf16[352,256]{1,0:T(8,128)(2,1)S(1)}, bf16[352,256]{1,0:T(8,128)(2,1)}, u32[]{:S(2)}) copy-start(bf16[352,256]{1,0:T(8,128)(2,1)} %constant.17.clone.row_matrix) | copy-start | bytes 540676
  18.7 2.0 %copy-start.2 = (bf16[192,1056]{1,0:T(8,128)(2,1)S(1)}, bf16[192,1056]{1,0:T(8,128)(2,1)}, u32[]{:S(2)}) copy-start(bf16[192,1056]{1,0:T(8,128)(2,1)} %constant.18.clone.spread_rows_0) | copy-start | bytes 1216516
  18.7 2.0 %copy-start.3 = (bf16[768,256]{1,0:T(8,128)(2,1)S(1)}, bf16[768,256]{1,0:T(8,128)(2,1)}, u32[]{:S(2)}) copy-start(bf16[768,256]{1,0:T(8,128)(2,1)} %constant.20.clone.spread_cols) | copy-start | bytes 1179652
  18.7 2.0 %copy-start.6 = (bf16[32,576]{1,0:T(8,128)(2,1)S(1)}, bf16[32,576]{1,0:T(8,128)(2,1)}, u32[]{:S(2)}) copy-start(bf16[32,576]{1,0:T(8,128)(2,1)} %constant.19.clone.spread_rows_1) | copy-start | bytes 110596

commit v3 on v2

--- a/solution.py
+++ b/solution.py
@@ -108,78 +108,76 @@
     return product(matrix, jnp.concatenate([high, low, high], axis=0))
 
 
-def transmit(
+def phases(
     plan,
-    part,
-    rows_ref,
-    cols_ref,
+    place_ref,
     main_ref,
     low_ref,
     high_ref,
-    row_matrix,
-    column_matrix,
-    cos_out,
-    sin_out,
-    strip,
-    patch,
+    table_ref,
+    cos_0,
+    sin_0,
+    cos_1,
+    sin_1,
+    strip_0,
+    strip_1,
+    patch_0,
+    patch_1,
 ):
-    f32 = jnp.float32
-    tiles = strip.shape[0]
-    grid_cols = tiles * LANES
+    f32, bf16 = jnp.float32, jnp.bfloat16
+    tiles = plan.grid_cols // LANES
+    span = plan.span
     strip_rows = main_ref.shape[1]
-    halo = (3 - part) * REACH
-    stored = patch.shape[0] * 2 // plan.probes
-    first_row, first_col = plan.origin()
+    strips, patches = (strip_0, strip_1), (patch_0, patch_1)
 
     def widen(tile, carry):
         lanes = pl.ds(pl.multiple_of(tile * LANES, LANES), LANES)
-        strip[tile, 0:PAD, :] = low_ref[:, lanes].astype(f32)
-        strip[tile, PAD : PAD + strip_rows, :] = main_ref[part, :, lanes].astype(f32)
-        strip[tile, PAD + strip_rows :, :] = high_ref[:, lanes].astype(f32)
+        at = tile * span
+        for part in range(2):
+            strips[part][pl.ds(at, PAD), :] = low_ref[part, :, lanes].astype(f32)
+            strips[part][pl.ds(at + PAD, strip_rows), :] = main_ref[part, :, lanes].astype(f32)
+            strips[part][pl.ds(at + PAD + strip_rows, PAD), :] = high_ref[part, :, lanes].astype(f32)
         return carry
 
     lax.fori_loop(0, tiles, widen, 0, unroll=4)
     lane = lax.broadcasted_iota(jnp.int32, (1, LANES), 1)
-
-    def window(probe, place):
-        row = rows_ref[probe] + (first_row + (PAD - halo))
-        start = cols_ref[probe] + (first_col + (grid_cols - halo))
-        start = jnp.where(start >= grid_cols, start - grid_cols, start)
-        tile = lax.shift_right_logical(start, 7)
-        offset = start & (LANES - 1)
-        beside = jnp.where(tile == tiles - 1, 0, tile + 1)
-        here = strip[tile, pl.ds(row, stored), :]
-        there = strip[beside, pl.ds(row, stored), :]
-        shift = (place + LANES - offset) & (LANES - 1)
-        return pltpu.roll(jnp.where(lane >= offset, here, there), shift, 1)
-
-    def gather(pair, carry):
-        probe = lax.shift_right_logical(pair, 3) * (2 * ROWS) + (pair & (ROWS - 1))
-        both = jnp.where(lane < HALF, window(probe, 0), window(probe + ROWS, HALF))
-        at = pl.ds(pl.multiple_of(pair * stored, ROWS), stored)
-        patch[at, :] = both.astype(patch.dtype)
-        return carry
-
-    lax.fori_loop(0, plan.probes // 2, gather, 0, unroll=8)
-
     cos_fit = fit(lambda t: np.cos(np.sqrt(t)), MIDDLE**2, 4)
     sin_fit = fit(lambda t: np.sinc(np.sqrt(t) / np.pi), MIDDLE**2, 4)
-    count = ROWS * stored
-    along = []
-    for group in range(0, plan.groups, 2):
-        counts = [patch[g * count : (g + 1) * count] for g in (group, group + 1)]
-        counts = jnp.concatenate([value.astype(jnp.bfloat16) for value in counts], axis=1)
-        both = product(row_matrix[...], counts)
-        half = both.shape[0] // 2
-        both = both[:half] + both[half:]
-        along += [both[:, :LANES], both[:, LANES:]]
-    phase = product(
-        jnp.concatenate(split(jnp.concatenate(along, axis=0)), axis=1), column_matrix[...]
-    )
-    phase = phase[:, :LANES] + (phase[:, LANES:] - MIDDLE)
-    square = phase * phase
-    cos_out[...] = horner(cos_fit, square)
-    sin_out[...] = phase * horner(sin_fit, square)
+    outs = ((cos_0, sin_0), (cos_1, sin_1))
+    tables = []
+    at = 0
+    for shape in plan.tables:
+        tables.append(table_ref[at : at + shape[0], : shape[1]])
+        at += shape[0]
+    for part in (1, 0):
+        strip, patch, stored = strips[part], patches[part], plan.stored[part]
+
+        def window(probe):
+            here, there, offset, shift = [place_ref[4 * part + i, probe] for i in range(4)]
+            both = jnp.where(
+                lane >= offset, strip[pl.ds(here, stored), :], strip[pl.ds(there, stored), :]
+            )
+            return pltpu.roll(both, shift, 1)
+
+        for pair in range(plan.probes // 2):
+            probe = pair // ROWS * 2 * ROWS + pair % ROWS
+            both = jnp.where(lane < HALF, window(probe), window(probe + ROWS))
+            patch[pair * stored : (pair + 1) * stored, :] = both.astype(patch.dtype)
+
+        count = ROWS * stored
+        size = plan.phase_rows[part] * ROWS
+        for group in range(0, plan.groups, 2):
+            counts = [patch[g * count : (g + 1) * count] for g in (group, group + 1)]
+            counts = jnp.concatenate([value.astype(bf16) for value in counts], axis=1)
+            both = product(tables[part], counts)
+            both = both[:size] + both[size:]
+            along = jnp.concatenate([both[:, :LANES], both[:, LANES:]], axis=0)
+            phase = product(jnp.concatenate(split(along), axis=1), tables[2])
+            phase = phase[:, :LANES] + (phase[:, LANES:] - MIDDLE)
+            square = phase * phase
+            cos_out, sin_out = outs[part]
+            cos_out[group * size : (group + 2) * size] = horner(cos_fit, square)
+            sin_out[group * size : (group + 2) * size] = phase * horner(sin_fit, square)
 
 
 def common_wave(plan, beam_ref, wave_ref):
@@ -228,12 +226,14 @@
 
 
 class Plan:
-    def __init__(self, grid_rows, grid_cols, beams, probes, pixels):
+    def __init__(self, grid_rows, grid_cols, beams, probes, pixels, span):
         self.grid_rows, self.grid_cols = grid_rows, grid_cols
         self.beams, self.probes, self.pixels = beams, probes, pixels
         self.groups = probes // (2 * ROWS)
         self.take_cols = min(pixels, CROP)
         self.take_rows = pixels // self.take_cols
+        self.halo = [3 * REACH, 2 * REACH]
+        self.span = span
         self.phase_rows = [self.take_rows + 4 * REACH, self.take_rows + 2 * REACH]
         self.stored = [-(-(count + 2 * REACH) // ROWS) * ROWS for count in self.phase_rows]
 
@@ -295,73 +295,80 @@
         beam_weight.shape[0] * beam_parts,
         probe_rows.shape[0],
         CROP * CROP // beam_parts,
-    )
-
-    forward = [(i, (i + 1) % tile_parts) for i in range(tile_parts)]
-    backward = [(target, source) for source, target in forward]
-    known = jnp.concatenate([beam_index.astype(jnp.float32), beam_weight[:, None]], axis=1)
+        strip_rows + 2 * PAD + 1,
+    )
+
+    f32, bf16 = jnp.float32, jnp.bfloat16
+    vmem = pl.BlockSpec(memory_space=pltpu.VMEM)
+    smem = pl.BlockSpec(memory_space=pltpu.SMEM)
+    params = pltpu.CompilerParams(vmem_limit_bytes=12 << 20)
+    tiles = grid_cols // LANES
+    known = jnp.concatenate([beam_index.astype(f32), beam_weight[:, None]], axis=1)
     known = jnp.pad(known, ((0, 0), (0, LANES - NUMBERS)))
-    edges = [
-        (atom_counts[part, strip_rows - PAD :], atom_counts[part, :PAD]) for part in range(2)
-    ]
-    known, edges = lax.optimization_barrier((known, edges))
 
     def share(known, reach):
         other = lax.ppermute(known, "beam", [(i, i ^ reach) for i in range(beam_parts)])
         return jnp.concatenate([known, other], axis=0)
 
-    halos = []
-    for part in range(2):
-        low = lax.ppermute(edges[part][0], "tile", forward)
-        high = lax.ppermute(edges[part][1], "tile", backward)
-        halos.append((low, high))
+    low = atom_counts[:, strip_rows - PAD :]
+    high = atom_counts[:, :PAD]
+
+    forward = [(i, (i + 1) % tile_parts) for i in range(tile_parts)]
+    backward = [(target, source) for source, target in forward]
+    low = lax.ppermute(low, "tile", forward)
+    high = lax.ppermute(high, "tile", backward)
     reach = 1
     while reach < beam_parts:
         known = share(known, reach)
         reach *= 2
 
-    f32, bf16 = jnp.float32, jnp.bfloat16
-    vmem = pl.BlockSpec(memory_space=pltpu.VMEM)
-    smem = pl.BlockSpec(memory_space=pltpu.SMEM)
-    phases = [(plan.groups * count * ROWS, LANES) for count in plan.phase_rows]
-    columns = jnp.asarray(column_blur())
-
-    def phase_call(part):
-        stored = plan.stored[part]
-        low, high = halos[part]
-        shape = jax.ShapeDtypeStruct(phases[part], f32)
+    first_row, first_col = plan.origin()
+    shape = (8, plan.probes)
+    which = lax.broadcasted_iota(jnp.int32, shape, 0)
+    halo = jnp.where(which < 4, plan.halo[0], plan.halo[1])
+    second = lax.broadcasted_iota(jnp.int32, shape, 1) // ROWS % 2 * HALF
+    row = probe_rows + (first_row + PAD - halo)
+    col = (probe_cols + (first_col + grid_cols - halo)) % grid_cols
+    tile, offset = col // LANES, col % LANES
+    beside = jnp.where(tile == tiles - 1, 0, tile + 1)
+    places = jnp.where(
+        which % 4 < 2,
+        jnp.where(which % 4 == 0, tile, beside) * plan.span + row,
+        jnp.where(which % 4 == 2, offset, (second + LANES - offset) % LANES),
+    )
+
+    shapes = [(plan.groups * count * ROWS, LANES) for count in plan.phase_rows]
+    shapes = [jax.ShapeDtypeStruct(shape, f32) for shape in shapes]
+    patches = []
+    for stored in plan.stored:
         kind = bf16 if stored % (2 * ROWS) == 0 else f32
-        call = pl.pallas_call(
-            functools.partial(transmit, plan, part),
-            out_shape=[shape, shape],
-            in_specs=[smem] * 2 + [vmem] * 5,
-            out_specs=[vmem] * 2,
-            scratch_shapes=[
-                pltpu.VMEM((grid_cols // LANES, strip_rows + 2 * PAD, LANES), f32),
-                pltpu.VMEM((plan.probes // 2 * stored, LANES), kind),
-            ],
-            compiler_params=pltpu.CompilerParams(vmem_limit_bytes=12 << 20),
-        )
-        matrix = jnp.asarray(row_blur(plan.phase_rows[part], stored))
-        return call(probe_rows, probe_cols, atom_counts, low, high, matrix, columns)
-
-    cos_1, sin_1 = phase_call(1)
-    cos_0, sin_0 = phase_call(0)
+        patches.append(pltpu.VMEM((plan.probes // 2 * stored, LANES), kind))
+    call = pl.pallas_call(
+        functools.partial(phases, plan),
+        out_shape=[shapes[0], shapes[0], shapes[1], shapes[1]],
+        in_specs=[smem] + [vmem] * 4,
+        out_specs=[vmem] * 4,
+        scratch_shapes=[pltpu.VMEM((tiles * plan.span, LANES), f32)] * 2 + patches,
+        compiler_params=params,
+        name="phases",
+    )
+    tables = [row_blur(plan.phase_rows[part], plan.stored[part]) for part in range(2)]
+    tables.append(column_blur())
+    plan.tables = [table.shape for table in tables]
+    width = max(cols for _, cols in plan.tables)
+    table = np.concatenate([np.pad(t, ((0, 0), (0, width - t.shape[1]))) for t in tables])
+    cos_0, sin_0, cos_1, sin_1 = call(places, atom_counts, low, high, jnp.asarray(table))
     call = pl.pallas_call(
         functools.partial(finish, plan),
         out_shape=jax.ShapeDtypeStruct((plan.pixels, plan.probes), f32),
         in_specs=[vmem] * 8,
         out_specs=vmem,
         scratch_shapes=[pltpu.VMEM((2, plan.phase_rows[0] * ROWS, LANES), f32)],
-        compiler_params=pltpu.CompilerParams(vmem_limit_bytes=12 << 20),
+        compiler_params=params,
         name="finish",
     )
-    matrices = [
-        row_spread(plan.phase_rows[1]),
-        row_spread(plan.take_rows),
-        column_spread(),
-    ]
-    out = call(known, cos_0, sin_0, cos_1, sin_1, *[jnp.asarray(m) for m in matrices])
+    tables = [row_spread(plan.phase_rows[1]), row_spread(plan.take_rows), column_spread()]
+    out = call(known, cos_0, sin_0, cos_1, sin_1, *[jnp.asarray(table) for table in tables])
     return out.T
 
 

time: 23.3 us -> 21 us (0.901)
  Pallas kernels: 6.05 us -> 4.13 us
  starting transfers between devices: 11.2 us -> 9.98 us
  local copies, waits for them, and re-layouts: 1.26 us -> 1.85 us
  waiting for transfers between devices: 3.46 us -> 3.87 us
    pallas_call x3 -> x2, Pallas kernels: 6.05 us -> 4.13 us  [the longest x1 2.24 us: window(): call(known, cos_0, sin_0, cos_1, sin_1, *[jnp.asarray(table) for table in...]
    squeeze x1 -> x0, local copies, waits for them, and re-layouts: 1.2 us -> none  [window(): atom_counts[part, :PAD]]
    slice x0 -> x1, local copies, waits for them, and re-layouts: none -> 1.15 us  [window(): high = atom_counts[:, :PAD]]
    ppermute x4 -> x2, starting transfers between devices: 3.49 us -> 2.56 us  [the longest x1 2.02 us: window(): high = lax.ppermute(high, 'tile', backward)]
    unnamed x20 -> x16, local copies, waits for them, and re-layouts: 0.06 us -> 0.7 us
    ppermute x3, waiting for transfers between devices: 3.45 us -> 3.87 us  [share(): lax.ppermute(known, 'beam', [(i, i ^ reach) for i in range(beam_parts)])]
    ppermute x3, starting transfers between devices: 7.73 us -> 7.41 us  [share(): lax.ppermute(known, 'beam', [(i, i ^ reach) for i in range(beam_parts)])]
  transfers between devices with their start and end apart: 7 -> 5, of which waited for: 2 -> 3; matrix products, arithmetic and copies ran while one was open for 0% -> 1% of each run, Pallas kernels for 8% -> 0%
where the time goes in v3:
time: 21 us; the launch traced here: 20.8 us
  starting transfers between devices  9.98 us (48%)
  Pallas kernels  4.13 us (20%)
  waiting for transfers between devices  3.87 us (18%)
  local copies, waits for them, and re-layouts  1.85 us (9%)
  between operations  0.78 us (4%)
  other arithmetic  0.22 us (1%)
    ppermute x3, starting transfers between devices, share(): lax.ppermute(known, 'beam', [(i, i ^ reach) for i in range(beam_parts)])  7.41 us
    ppermute x3, waiting for transfers between devices, share(): lax.ppermute(known, 'beam', [(i, i ^ reach) for i in range(beam_parts)])  3.87 us
    pallas_call x1, Pallas kernels, window(): call(known, cos_0, sin_0, cos_1, sin_1, *[jnp.asarray(table) for table in...  2.24 us
    ppermute x1, starting transfers between devices, window(): high = lax.ppermute(high, 'tile', backward)  2.02 us
    pallas_call x1, Pallas kernels, window(): call(places, atom_counts, low, high, jnp.asarray(table))  1.89 us
    slice x1, local copies, waits for them, and re-layouts, window(): high = atom_counts[:, :PAD]  1.15 us
    unnamed x16, local copies, waits for them, and re-layouts  0.7 us
    ppermute x1, starting transfers between devices, window(): low = lax.ppermute(low, 'tile', forward)  0.55 us
  transfers between devices with their start and end apart: 5, of which 3 were waited for; matrix products, arithmetic and copies ran while one was open for 1% of the time, Pallas kernels for 0%

profile of v3, /device:TPU:0, one launch (start us, length us, event | category | flops | bytes accessed | tf_op | source)
XLA Modules:
  0.0 20.8 jit_solution(10392331698291924761)
XLA Ops:
  0.0 0.0 copy-start.2
  0.0 0.0 copy-start
  0.0 1.1 %fusion.12 = (bf16[2,16,4096]{2,1,0:T(8,128)(2,1)S(1)}, bf16[2,16,4096]{2,1,0:T(8,128)(2,1)S(1)}) fusion(bf16[2,32,4096]{2,1,0:T(8,128)(2,1)} %main_ref.1), kind=kLoop, calls=%fused_computation.48 | loop fusion | bytes 1048576 | tf_op jit(solution)/shard_map/slice | solution.py:314
  1.2 0.5 %collective-permute-start.3 = (bf16[2,16,4096]{2,1,0:T(8,128)(2,1)S(1)}, bf16[2,16,4096]{2,1,0:T(8,128)(2,1)S(1)}, u32[]{:S(2)}, u32[]{:S(2)}) collective-permute-start(bf16[2,16,4096]{2,1,0:T(8,128)(2,1)S(1)} %get-tuple-element.14), channel_id=1, source_target_pairs={{0,1},{1,2},{2,3},{3,0},{4,5},{5,6},{6,7},{7,4},{8,9},{9,10},{10,1... | collective-permute-start | bytes 786440 | tf_op jit(solution)/shard_map/ppermute | solution.py:318
  1.7 0.0 copy-start.7
  1.7 2.0 %collective-permute-start.4 = (bf16[2,16,4096]{2,1,0:T(8,128)(2,1)S(1)}, bf16[2,16,4096]{2,1,0:T(8,128)(2,1)S(1)}, u32[]{:S(2)}, u32[]{:S(2)}) collective-permute-start(bf16[2,16,4096]{2,1,0:T(8,128)(2,1)S(1)} %get-tuple-element.13), channel_id=1, source_target_pairs={{1,0},{2,1},{3,2},{0,3},{5,4},{6,5},{7,6},{4,7},{9,8},{10,9},{11,1... | collective-permute-start | bytes 786440 | tf_op jit(solution)/shard_map/ppermute | solution.py:319
  4.4 0.0 copy-done.7
  4.4 0.1 fusion.9
  4.5 2.2 %collective-permute-start = (f32[1,128]{1,0:T(1,128)S(1)}, f32[1,128]{1,0:T(1,128)S(1)}, u32[]{:S(2)}, u32[]{:S(2)}) collective-permute-start(f32[1,128]{1,0:T(1,128)S(1)} %fusion.9), channel_id=1, source_target_pairs={{0,4},{4,0},{8,12},{12,8},{16,20},{20,16},{24,28},{28,24},{1,5},{5... | collective-permute-start | bytes 1544 | tf_op jit(solution)/shard_map/ppermute | solution.py:310
  6.7 1.5 %collective-permute-done = f32[1,128]{1,0:T(1,128)S(1)} collective-permute-done((f32[1,128]{1,0:T(1,128)S(1)}, f32[1,128]{1,0:T(1,128)S(1)}, u32[]{:S(2)}, u32[]{:S(2)}) %collective-permute-start) | collective-permute-done | bytes 544 | tf_op jit(solution)/shard_map/ppermute | solution.py:310
  8.2 2.1 %collective-permute-start.1 = (f32[2,128]{1,0:T(2,128)S(1)}, f32[2,128]{1,0:T(2,128)S(1)}, u32[]{:S(2)}, u32[]{:S(2)}) collective-permute-start(f32[2,128]{1,0:T(2,128)S(1)} %pad_maximum_fusion.2), channel_id=1, source_target_pairs={{0,8},{4,12},{8,0},{12,4},{16,24},{20,28},{24,16},{28,20},{1,9},{5... | collective-permute-start | bytes 3080 | tf_op jit(solution)/shard_map/ppermute | solution.py:310
  10.3 1.5 %collective-permute-done.1 = f32[2,128]{1,0:T(2,128)S(1)} collective-permute-done((f32[2,128]{1,0:T(2,128)S(1)}, f32[2,128]{1,0:T(2,128)S(1)}, u32[]{:S(2)}, u32[]{:S(2)}) %collective-permute-start.1) | collective-permute-done | bytes 1056 | tf_op jit(solution)/shard_map/ppermute | solution.py:310
  11.9 3.1 %collective-permute-start.2 = (f32[4,128]{1,0:T(4,128)S(1)}, f32[4,128]{1,0:T(4,128)S(1)}, u32[]{:S(2)}, u32[]{:S(2)}) collective-permute-start(f32[4,128]{1,0:T(4,128)S(1)} %pad_maximum_fusion.1), channel_id=1, source_target_pairs={{0,16},{4,20},{8,24},{12,28},{16,0},{20,4},{24,8},{28,12},{1,17},{... | collective-permute-start | bytes 6152 | tf_op jit(solution)/shard_map/ppermute | solution.py:310
  15.0 0.0 copy-start.5
  15.0 0.0 copy-start.6
  15.0 0.7 %copy-done.5 = s32[64]{0:T(128)S(1)} copy-done((s32[64]{0:T(128)S(1)}, s32[64]{0:T(128)}, u32[]{:S(2)}) %copy-start.5) | copy-done | bytes 280
  15.7 0.0 copy-done.6
  15.7 0.1 fusion.5.place_ref
  15.8 0.8 %collective-permute-done.2 = f32[4,128]{1,0:T(4,128)S(1)} collective-permute-done((f32[4,128]{1,0:T(4,128)S(1)}, f32[4,128]{1,0:T(4,128)S(1)}, u32[]{:S(2)}, u32[]{:S(2)}) %collective-permute-start.2) | collective-permute-done | bytes 2080 | tf_op jit(solution)/shard_map/ppermute | solution.py:310
  16.6 0.0 copy-start.1
  16.6 0.0 copy-start.3
  16.6 0.0 copy-start.4
  16.6 0.0 collective-permute-done.3.low_ref
  16.6 0.0 collective-permute-done.4.high_ref
  16.6 0.0 copy-done.2
  16.6 0.0 copy-done
  16.7 1.9 %phases.1 = (f32[704,128]{1,0:T(8,128)S(1)}, f32[704,128]{1,0:T(8,128)S(1)}, f32[384,128]{1,0:T(8,128)S(1)}, f32[384,128]{1,0:T(8,128)S(1)}) custom-call(s32[8,64]{1,0:T(8,128)S(1)} %fusion.5.place_ref, bf16[2,32,4096]{2,1,0:T(8,128)(2,1)S(1)} %copy-done, bf16[2,16,4096]{2,1,0:T(8,128)(2,1)S(1)} %collective-permute-done.3.low_ref, ...), custom_call_target="tpu_custom_call" | custom-call | tf_op jit(solution)/shard_map/phases/pallas_call | solution.py:360
  18.6 0.0 copy-done.1
  18.6 0.0 copy-done.3
  18.6 0.0 copy-done.4
  18.6 2.2 %finish.1 = f32[32,64]{1,0:T(8,128)} custom-call(f32[8,128]{1,0:T(8,128)S(1)} %pad_maximum_fusion.beam_ref, f32[704,128]{1,0:T(8,128)S(1)} %get-tuple-element.9.cos_0, f32[704,128]{1,0:T(8,128)S(1)} %get-tuple-element.10.sin_0, f32[384,128]{1,0:T(8,128)S(1)} %get-tuple-element.11.cos_1, f32[384,128]{1,0:T(8,128)S(1)} %get-tuple-element.12.sin_1, ...), custom_call_target="tpu_custom_call" | custom-call | tf_op jit(solution)/shard_map/finish/pallas_call | solution.py:371
  (9 shorter events, 0.1 us)
Async XLA Ops:
  0.0 16.6 %copy-start.2 = (bf16[800,256]{1,0:T(8,128)(2,1)S(1)}, bf16[800,256]{1,0:T(8,128)(2,1)}, u32[]{:S(2)}) copy-start(bf16[800,256]{1,0:T(8,128)(2,1)} %constant.140.clone.table_ref) | copy-start | bytes 1228804
  0.0 16.6 %copy-start = (bf16[2,32,4096]{2,1,0:T(8,128)(2,1)S(1)}, bf16[2,32,4096]{2,1,0:T(8,128)(2,1)}, u32[]{:S(2)}) copy-start(bf16[2,32,4096]{2,1,0:T(8,128)(2,1)} %main_ref.1) | copy-start | bytes 1572868
  1.2 15.5 %collective-permute-start.3 = (bf16[2,16,4096]{2,1,0:T(8,128)(2,1)S(1)}, bf16[2,16,4096]{2,1,0:T(8,128)(2,1)S(1)}, u32[]{:S(2)}, u32[]{:S(2)}) collective-permute-start(bf16[2,16,4096]{2,1,0:T(8,128)(2,1)S(1)} %get-tuple-element.14), channel_id=1, source_target_pairs={{0,1},{1,2},{2,3},{3,0},{4,5},{5,6},{6,7},{7,4},{8,9},{9,10},{10,1... | collective-permute-start | bytes 786440 | tf_op jit(solution)/shard_map/ppermute | solution.py:318
  1.7 2.7 %copy-start.7 = (s32[1,2]{1,0:T(1,128)S(1)}, s32[1,2]{1,0:T(1,128)}, u32[]{:S(2)}) copy-start(s32[1,2]{1,0:T(1,128)} %param.10) | copy-start | bytes 28
  1.7 14.9 %collective-permute-start.4 = (bf16[2,16,4096]{2,1,0:T(8,128)(2,1)S(1)}, bf16[2,16,4096]{2,1,0:T(8,128)(2,1)S(1)}, u32[]{:S(2)}, u32[]{:S(2)}) collective-permute-start(bf16[2,16,4096]{2,1,0:T(8,128)(2,1)S(1)} %get-tuple-element.13), channel_id=1, source_target_pairs={{1,0},{2,1},{3,2},{0,3},{5,4},{6,5},{7,6},{4,7},{9,8},{10,9},{11,1... | collective-permute-start | bytes 786440 | tf_op jit(solution)/shard_map/ppermute | solution.py:319
  4.5 3.8 %collective-permute-start = (f32[1,128]{1,0:T(1,128)S(1)}, f32[1,128]{1,0:T(1,128)S(1)}, u32[]{:S(2)}, u32[]{:S(2)}) collective-permute-start(f32[1,128]{1,0:T(1,128)S(1)} %fusion.9), channel_id=1, source_target_pairs={{0,4},{4,0},{8,12},{12,8},{16,20},{20,16},{24,28},{28,24},{1,5},{5... | collective-permute-start | bytes 1544 | tf_op jit(solution)/shard_map/ppermute | solution.py:310
  8.2 3.7 %collective-permute-start.1 = (f32[2,128]{1,0:T(2,128)S(1)}, f32[2,128]{1,0:T(2,128)S(1)}, u32[]{:S(2)}, u32[]{:S(2)}) collective-permute-start(f32[2,128]{1,0:T(2,128)S(1)} %pad_maximum_fusion.2), channel_id=1, source_target_pairs={{0,8},{4,12},{8,0},{12,4},{16,24},{20,28},{24,16},{28,20},{1,9},{5... | collective-permute-start | bytes 3080 | tf_op jit(solution)/shard_map/ppermute | solution.py:310
  11.9 4.7 %collective-permute-start.2 = (f32[4,128]{1,0:T(4,128)S(1)}, f32[4,128]{1,0:T(4,128)S(1)}, u32[]{:S(2)}, u32[]{:S(2)}) collective-permute-start(f32[4,128]{1,0:T(4,128)S(1)} %pad_maximum_fusion.1), channel_id=1, source_target_pairs={{0,16},{4,20},{8,24},{12,28},{16,0},{20,4},{24,8},{28,12},{1,17},{... | collective-permute-start | bytes 6152 | tf_op jit(solution)/shard_map/ppermute | solution.py:310
  15.0 0.7 %copy-start.5 = (s32[64]{0:T(128)S(1)}, s32[64]{0:T(128)}, u32[]{:S(2)}) copy-start(s32[64]{0:T(128)} %param.12) | copy-start | bytes 772
  15.0 0.7 %copy-start.6 = (s32[64]{0:T(128)S(1)}, s32[64]{0:T(128)}, u32[]{:S(2)}) copy-start(s32[64]{0:T(128)} %param.13) | copy-start | bytes 772
  16.6 2.0 %copy-start.1 = (bf16[192,1056]{1,0:T(8,128)(2,1)S(1)}, bf16[192,1056]{1,0:T(8,128)(2,1)}, u32[]{:S(2)}) copy-start(bf16[192,1056]{1,0:T(8,128)(2,1)} %constant.141.clone.spread_rows_0) | copy-start | bytes 1216516
  16.6 2.0 %copy-start.3 = (bf16[768,256]{1,0:T(8,128)(2,1)S(1)}, bf16[768,256]{1,0:T(8,128)(2,1)}, u32[]{:S(2)}) copy-start(bf16[768,256]{1,0:T(8,128)(2,1)} %constant.143.clone.spread_cols) | copy-start | bytes 1179652
  16.6 2.0 %copy-start.4 = (bf16[32,576]{1,0:T(8,128)(2,1)S(1)}, bf16[32,576]{1,0:T(8,128)(2,1)}, u32[]{:S(2)}) copy-start(bf16[32,576]{1,0:T(8,128)(2,1)} %constant.142.clone.spread_rows_1) | copy-start | bytes 110596

commit v4 on v3

--- a/solution.py
+++ b/solution.py
@@ -16,6 +16,7 @@
 HALF = 64
 ROWS = 8
 PAD = 16
+NEAR = 8
 PHASE = 0.6
 MIDDLE = 1.2
 NUMBERS = 3
@@ -56,8 +57,7 @@
     _, real, imag = make_taps()
     real, imag = band(real, count), band(imag, count)
     taps = np.block([[real, -imag], [imag, real]])
-    high, low = two_parts(np.kron(taps, np.eye(ROWS)))
-    return np.concatenate([high, high, low], axis=1)
+    return np.concatenate(two_parts(np.kron(taps, np.eye(ROWS))), axis=0)
 
 
 def column_band(taps):
@@ -72,14 +72,21 @@
 def column_spread():
     _, real, imag = make_taps()
     real, imag = column_band(real), column_band(imag)
-    high, low = two_parts(np.block([[real, imag], [-imag, real]]))
-    return np.concatenate([high, high, low], axis=0)
+    return np.concatenate(two_parts(np.block([[real, imag], [-imag, real]])), axis=0)
 
 
 def fit(function, top, degree):
     nodes = top / 2 * (1 + np.cos(np.pi * (np.arange(200) + 0.5) / 200))
     series = np.polynomial.Chebyshev.fit(nodes, function(nodes), degree, domain=[0, top])
     return [float(c) for c in series.convert(kind=np.polynomial.Polynomial).coef]
+
+
+def ROUNDS(count):
+    reaches = []
+    while count > 1:
+        count //= 2
+        reaches.append(count)
+    return reaches[::-1]
 
 
 def horner(coefficients, value):
@@ -99,21 +106,60 @@
 
 
 def column_product(value, matrix):
+    count, half = value.shape[0], matrix.shape[0] // 2
     high, low = split(value)
-    return product(jnp.concatenate([high, low, high], axis=1), matrix)
+    both = product(jnp.concatenate([high, low], axis=0), matrix[:half])
+    return both[:count] + both[count:] + product(high, matrix[half:])
 
 
 def row_product(matrix, value):
+    half = matrix.shape[0] // 2
     high, low = split(value)
-    return product(matrix, jnp.concatenate([high, low, high], axis=0))
+    both = product(matrix, high)
+    return both[:half] + both[half:] + product(matrix[:half], low)
+
+
+def choose(plan, top_ref, bottom_ref, rows_ref, cols_ref, _, far_ref, near_ref, place_ref):
+    find_places(plan, rows_ref, cols_ref, place_ref)
+    first = lax.axis_index("beam") < lax.axis_size("beam") // 2
+
+    @pl.when(first)
+    def _():
+        far_ref[...] = bottom_ref[...]
+        near_ref[...] = top_ref[:, :NEAR, :]
+
+    @pl.when(jnp.logical_not(first))
+    def _():
+        far_ref[...] = top_ref[...]
+        near_ref[...] = bottom_ref[:, PAD - NEAR :, :]
+
+
+def find_places(plan, rows_ref, cols_ref, place_ref):
+    grid_cols = plan.grid_cols
+    first_row, first_col = plan.origin()
+    shape = place_ref.shape
+    which = lax.broadcasted_iota(jnp.int32, shape, 0)
+    halo = jnp.where(which < 4, plan.halo[0], plan.halo[1])
+    which = which & 3
+    second = (lax.broadcasted_iota(jnp.int32, shape, 1) & ROWS) * (HALF // ROWS)
+    row = rows_ref[...] + (first_row + PAD - halo)
+    col = cols_ref[...] + (first_col + grid_cols - halo)
+    col = jnp.where(col >= grid_cols, col - grid_cols, col)
+    tile, offset = lax.shift_right_logical(col, 7), col & (LANES - 1)
+    beside = jnp.where(tile == grid_cols // LANES - 1, 0, tile + 1)
+    place_ref[...] = jnp.where(
+        which < 2,
+        jnp.where(which == 0, tile, beside) * plan.span + row,
+        jnp.where(which == 2, offset, (second + LANES - offset) & (LANES - 1)),
+    )
 
 
 def phases(
     plan,
     place_ref,
     main_ref,
-    low_ref,
-    high_ref,
+    far_ref,
+    near_ref,
     table_ref,
     cos_0,
     sin_0,
@@ -129,14 +175,17 @@
     span = plan.span
     strip_rows = main_ref.shape[1]
     strips, patches = (strip_0, strip_1), (patch_0, patch_1)
+    first = lax.axis_index("beam") < lax.axis_size("beam") // 2
+    far_at = jnp.where(first, 0, PAD + strip_rows)
+    near_at = jnp.where(first, PAD + strip_rows, PAD - NEAR)
 
     def widen(tile, carry):
         lanes = pl.ds(pl.multiple_of(tile * LANES, LANES), LANES)
         at = tile * span
         for part in range(2):
-            strips[part][pl.ds(at, PAD), :] = low_ref[part, :, lanes].astype(f32)
+            strips[part][pl.ds(at + far_at, PAD), :] = far_ref[part, :, lanes].astype(f32)
             strips[part][pl.ds(at + PAD, strip_rows), :] = main_ref[part, :, lanes].astype(f32)
-            strips[part][pl.ds(at + PAD + strip_rows, PAD), :] = high_ref[part, :, lanes].astype(f32)
+            strips[part][pl.ds(at + near_at, NEAR), :] = near_ref[part, :, lanes].astype(f32)
         return carry
 
     lax.fori_loop(0, tiles, widen, 0, unroll=4)
@@ -184,8 +233,7 @@
     f32 = jnp.float32
     count = wave_ref.shape[1] // ROWS
     shape = (-(-count // ROWS) * ROWS, LANES)
-    beams = beam_ref[...]
-    turn_fit = fit(lambda t: np.cos(2 * np.pi * np.sqrt(t)), 0.25, 9)
+    turn_fit = fit(lambda t: 2 * np.pi * np.sinc(2 * np.sqrt(t)), 0.0625, 5)
     first_row, first_col = plan.origin()
     dx = lax.broadcasted_iota(jnp.int32, shape, 0) + (first_row - 2 * REACH)
     lane = lax.broadcasted_iota(jnp.int32, shape, 1)
@@ -195,13 +243,15 @@
     dy = dy.astype(f32) * (1.0 / plan.grid_cols)
     quarter = jnp.where(upper, 0.25, 0.0).astype(f32)
 
+    numbers = [
+        jnp.broadcast_to(beam_ref[:, i : i + 1], (plan.beams, LANES)) for i in range(NUMBERS)
+    ]
     both = jnp.zeros(shape, f32)
     for beam in range(plan.beams):
-        row, col, weight = [beams[beam : beam + 1, i : i + 1] for i in range(NUMBERS)]
-        turns = row * dx + col * dy
-        turns = turns - jnp.round(turns) - quarter
-        turns = turns - jnp.round(turns)
-        both = both + weight * horner(turn_fit, turns * turns)
+        row, col, weight = [number[beam : beam + 1] for number in numbers]
+        turns = row * dx + (col * dy - quarter)
+        left = 0.25 - jnp.abs(turns - jnp.round(turns))
+        both = both + (weight * left) * horner(turn_fit, left * left)
     turned = pltpu.roll(both, HALF, 1)
     real = jnp.where(upper, turned, both)
     imag = jnp.where(upper, both, turned)
@@ -287,7 +337,7 @@
 
 
 def window(atom_counts, beam_index, beam_weight, probe_rows, probe_cols):
-    _, strip_rows, grid_cols = atom_counts.shape
+    slices, strip_rows, grid_cols = atom_counts.shape
     beam_parts, tile_parts = lax.axis_size("beam"), lax.axis_size("tile")
     plan = Plan(
         strip_rows * tile_parts,
@@ -306,36 +356,39 @@
     known = jnp.concatenate([beam_index.astype(f32), beam_weight[:, None]], axis=1)
     known = jnp.pad(known, ((0, 0), (0, LANES - NUMBERS)))
 
-    def share(known, reach):
+    top, bottom = atom_counts[:, :PAD], atom_counts[:, strip_rows - PAD :]
+    tables = [row_blur(plan.phase_rows[part], plan.stored[part]) for part in range(2)]
+    tables.append(column_blur())
+    plan.tables = [table.shape for table in tables]
+    width = max(cols for _, cols in plan.tables)
+    table = np.concatenate([np.pad(t, ((0, 0), (0, width - t.shape[1]))) for t in tables])
+    table = jnp.asarray(table)
+    far, near, places = pl.pallas_call(
+        functools.partial(choose, plan),
+        out_shape=[
+            jax.ShapeDtypeStruct((slices, PAD, grid_cols), bf16),
+            jax.ShapeDtypeStruct((slices, NEAR, grid_cols), bf16),
+            jax.ShapeDtypeStruct((8, plan.probes), jnp.int32),
+        ],
+        in_specs=[vmem] * 5,
+        out_specs=[vmem] * 3,
+        compiler_params=pltpu.CompilerParams(vmem_limit_bytes=2 << 20),
+        name="choose",
+    )(top, bottom, probe_rows[None], probe_cols[None], table)
+
+    def pass_on(rows, step):
+        pairs = []
+        for beam in range(beam_parts):
+            move = step if beam < beam_parts // 2 else -step
+            for tile in range(tile_parts):
+                pairs.append((beam * tile_parts + tile, beam * tile_parts + (tile + move) % tile_parts))
+        return lax.ppermute(rows, ("beam", "tile"), pairs)
+
+    far = pass_on(far, 1)
+    near = pass_on(near, -1)
+    for reach in ROUNDS(beam_parts):
         other = lax.ppermute(known, "beam", [(i, i ^ reach) for i in range(beam_parts)])
-        return jnp.concatenate([known, other], axis=0)
-
-    low = atom_counts[:, strip_rows - PAD :]
-    high = atom_counts[:, :PAD]
-
-    forward = [(i, (i + 1) % tile_parts) for i in range(tile_parts)]
-    backward = [(target, source) for source, target in forward]
-    low = lax.ppermute(low, "tile", forward)
-    high = lax.ppermute(high, "tile", backward)
-    reach = 1
-    while reach < beam_parts:
-        known = share(known, reach)
-        reach *= 2
-
-    first_row, first_col = plan.origin()
-    shape = (8, plan.probes)
-    which = lax.broadcasted_iota(jnp.int32, shape, 0)
-    halo = jnp.where(which < 4, plan.halo[0], plan.halo[1])
-    second = lax.broadcasted_iota(jnp.int32, shape, 1) // ROWS % 2 * HALF
-    row = probe_rows + (first_row + PAD - halo)
-    col = (probe_cols + (first_col + grid_cols - halo)) % grid_cols
-    tile, offset = col // LANES, col % LANES
-    beside = jnp.where(tile == tiles - 1, 0, tile + 1)
-    places = jnp.where(
-        which % 4 < 2,
-        jnp.where(which % 4 == 0, tile, beside) * plan.span + row,
-        jnp.where(which % 4 == 2, offset, (second + LANES - offset) % LANES),
-    )
+        known = jnp.concatenate([known, other], axis=0)
 
     shapes = [(plan.groups * count * ROWS, LANES) for count in plan.phase_rows]
     shapes = [jax.ShapeDtypeStruct(shape, f32) for shape in shapes]
@@ -352,12 +405,7 @@
         compiler_params=params,
         name="phases",
     )
-    tables = [row_blur(plan.phase_rows[part], plan.stored[part]) for part in range(2)]
-    tables.append(column_blur())
-    plan.tables = [table.shape for table in tables]
-    width = max(cols for _, cols in plan.tables)
-    table = np.concatenate([np.pad(t, ((0, 0), (0, width - t.shape[1]))) for t in tables])
-    cos_0, sin_0, cos_1, sin_1 = call(places, atom_counts, low, high, jnp.asarray(table))
+    cos_0, sin_0, cos_1, sin_1 = call(places, atom_counts, far, near, table)
     call = pl.pallas_call(
         functools.partial(finish, plan),
         out_shape=jax.ShapeDtypeStruct((plan.pixels, plan.probes), f32),

time: 21 us -> 18.1 us (0.86)
  waiting for transfers between devices: 3.87 us -> 2.71 us
  starting transfers between devices: 9.98 us -> 8.97 us
  local copies, waits for them, and re-layouts: 1.85 us -> 1.13 us
    ppermute x5, waiting for transfers between devices: 3.87 us -> 2.71 us  [the longest x3 2.7 us: window(): lax.ppermute(known, 'beam', [(i, i ^ reach) for i in range(beam_parts)])]
    ppermute x5, starting transfers between devices: 9.98 us -> 8.97 us  [the longest x3 8.21 us: window(): lax.ppermute(known, 'beam', [(i, i ^ reach) for i in range(beam_parts)])]
    unnamed x16, local copies, waits for them, and re-layouts: 0.7 us -> 0.04 us
    pallas_call x1 -> x2, Pallas kernels: 1.89 us -> 1.92 us  [the longest x1 1.87 us: window(): cos_0, sin_0, cos_1, sin_1 = call(places, atom_counts, far, near, table)]
  transfers between devices with their start and end apart: 5 -> 5, of which waited for: 3 -> 3; matrix products, arithmetic and copies ran while one was open for 1% -> 6% of each run, Pallas kernels for 0% -> 0%
where the time goes in v4:
time: 18.1 us; the launch traced here: 17.9 us
  starting transfers between devices  8.97 us (50%)
  Pallas kernels  4.19 us (23%)
  waiting for transfers between devices  2.71 us (15%)
  local copies, waits for them, and re-layouts  1.13 us (6%)
  between operations  0.82 us (5%)
    ppermute x3, starting transfers between devices, window(): lax.ppermute(known, 'beam', [(i, i ^ reach) for i in range(beam_parts)])  8.21 us
    ppermute x3, waiting for transfers between devices, window(): lax.ppermute(known, 'beam', [(i, i ^ reach) for i in range(beam_parts)])  2.7 us
    pallas_call x1, Pallas kernels, window(): call(known, cos_0, sin_0, cos_1, sin_1, *[jnp.asarray(table) for table in...  2.27 us
    pallas_call x1, Pallas kernels, window(): cos_0, sin_0, cos_1, sin_1 = call(places, atom_counts, far, near, table)  1.87 us
    slice x1, local copies, waits for them, and re-layouts, window(): top, bottom = (atom_counts[:, :PAD], atom_counts[:, strip_rows - PAD:])  1.09 us
    ppermute x2, starting transfers between devices, pass_on(): return lax.ppermute(rows, ('beam', 'tile'), pairs)  0.76 us
  transfers between devices with their start and end apart: 5, of which 3 were waited for; matrix products, arithmetic and copies ran while one was open for 6% of the time, Pallas kernels for 0%

profile of v4, /device:TPU:0, one launch (start us, length us, event | category | flops | bytes accessed | tf_op | source)
XLA Modules:
  0.0 17.9 jit_solution(12274454828450112496)
XLA Ops:
  0.0 0.0 copy-start.7
  0.7 0.0 copy-done.7
  0.7 0.1 fusion
  0.8 0.0 copy-start.1
  0.8 3.0 %collective-permute-start = (f32[1,128]{1,0:T(1,128)S(1)}, f32[1,128]{1,0:T(1,128)S(1)}, u32[]{:S(2)}, u32[]{:S(2)}) collective-permute-start(f32[1,128]{1,0:T(1,128)S(1)} %fusion), channel_id=1, source_target_pairs={{0,4},{4,0},{8,12},{12,8},{16,20},{20,16},{24,28},{28,24},{1,5},{5... | collective-permute-start | bytes 1544 | tf_op jit(solution)/shard_map/ppermute | solution.py:390
  3.8 0.0 copy-start.5
  3.8 0.0 copy-start.6
  3.8 1.1 %fusion.1 = (bf16[2,16,4096]{2,1,0:T(8,128)(2,1)S(1)}, bf16[2,16,4096]{2,1,0:T(8,128)(2,1)S(1)}) fusion(bf16[2,32,4096]{2,1,0:T(8,128)(2,1)} %main_ref.1), kind=kLoop, calls=%fused_computation.6 | loop fusion | bytes 1048576 | tf_op jit(solution)/shard_map/slice | solution.py:359
  4.8 0.0 copy-start
  4.9 0.0 copy-done.1
  4.9 0.0 copy-done.5
  4.9 0.0 copy-done.6
  4.9 0.1 collective-permute-start.3
  5.0 0.3 %collective-permute-done = f32[1,128]{1,0:T(1,128)S(1)} collective-permute-done((f32[1,128]{1,0:T(1,128)S(1)}, f32[1,128]{1,0:T(1,128)S(1)}, u32[]{:S(2)}, u32[]{:S(2)}) %collective-permute-start) | collective-permute-done | bytes 544 | tf_op jit(solution)/shard_map/ppermute | solution.py:390
  5.3 2.1 %collective-permute-start.1 = (f32[2,128]{1,0:T(2,128)S(1)}, f32[2,128]{1,0:T(2,128)S(1)}, u32[]{:S(2)}, u32[]{:S(2)}) collective-permute-start(f32[2,128]{1,0:T(2,128)S(1)} %pad_maximum_fusion.2), channel_id=1, source_target_pairs={{0,8},{4,12},{8,0},{12,4},{16,24},{20,28},{24,16},{28,20},{1,9},{5... | collective-permute-start | bytes 3080 | tf_op jit(solution)/shard_map/ppermute | solution.py:390
  7.4 0.7 %collective-permute-start.4 = (bf16[2,8,4096]{2,1,0:T(8,128)(2,1)S(1)}, bf16[2,8,4096]{2,1,0:T(8,128)(2,1)S(1)}, u32[]{:S(2)}, u32[]{:S(2)}) collective-permute-start(bf16[2,8,4096]{2,1,0:T(8,128)(2,1)S(1)} %get-tuple-element.14), channel_id=1, source_target_pairs={{0,3},{1,0},{2,1},{3,2},{4,7},{5,4},{6,5},{7,6},{8,11},{9,8},{10,9... | collective-permute-start | bytes 393224 | tf_op jit(solution)/shard_map/ppermute | solution.py:385
  8.1 0.8 %collective-permute-done.1 = f32[2,128]{1,0:T(2,128)S(1)} collective-permute-done((f32[2,128]{1,0:T(2,128)S(1)}, f32[2,128]{1,0:T(2,128)S(1)}, u32[]{:S(2)}, u32[]{:S(2)}) %collective-permute-start.1) | collective-permute-done | bytes 1056 | tf_op jit(solution)/shard_map/ppermute | solution.py:390
  9.0 3.1 %collective-permute-start.2 = (f32[4,128]{1,0:T(4,128)S(1)}, f32[4,128]{1,0:T(4,128)S(1)}, u32[]{:S(2)}, u32[]{:S(2)}) collective-permute-start(f32[4,128]{1,0:T(4,128)S(1)} %pad_maximum_fusion.1), channel_id=1, source_target_pairs={{0,16},{4,20},{8,24},{12,28},{16,0},{20,4},{24,8},{28,12},{1,17},{... | collective-permute-start | bytes 6152 | tf_op jit(solution)/shard_map/ppermute | solution.py:390
  12.1 1.6 %collective-permute-done.2 = f32[4,128]{1,0:T(4,128)S(1)} collective-permute-done((f32[4,128]{1,0:T(4,128)S(1)}, f32[4,128]{1,0:T(4,128)S(1)}, u32[]{:S(2)}, u32[]{:S(2)}) %collective-permute-start.2) | collective-permute-done | bytes 2080 | tf_op jit(solution)/shard_map/ppermute | solution.py:390
  13.7 0.0 collective-permute-done.4.near_ref
  13.7 0.0 collective-permute-done.3.far_ref
  13.7 0.0 copy-done
  13.7 0.0 copy-start.2
  13.7 0.0 copy-start.3
  13.7 0.0 copy-start.4
  13.7 1.9 %phases.1 = (f32[704,128]{1,0:T(8,128)S(1)}, f32[704,128]{1,0:T(8,128)S(1)}, f32[384,128]{1,0:T(8,128)S(1)}, f32[384,128]{1,0:T(8,128)S(1)}) custom-call(s32[8,64]{1,0:T(8,128)S(1)} %get-tuple-element.12.place_ref, bf16[2,32,4096]{2,1,0:T(8,128)(2,1)S(1)} %copy-done, bf16[2,16,4096]{2,1,0:T(8,128)(2,1)S(1)} %collective-permute-done.3.far_ref, ...), custom_call_target="tpu_custom_call" | custom-call | tf_op jit(solution)/shard_map/phases/pallas_call | solution.py:408
  15.6 0.0 copy-done.2
  15.6 0.0 copy-done.3
  15.6 0.0 copy-done.4
  15.7 2.3 %finish.1 = f32[32,64]{1,0:T(8,128)} custom-call(f32[8,128]{1,0:T(8,128)S(1)} %pad_maximum_fusion.beam_ref, f32[704,128]{1,0:T(8,128)S(1)} %get-tuple-element.15.cos_0, f32[704,128]{1,0:T(8,128)S(1)} %get-tuple-element.16.sin_0, f32[384,128]{1,0:T(8,128)S(1)} %get-tuple-element.17.cos_1, f32[384,128]{1,0:T(8,128)S(1)} %get-tuple-element.18.sin_1, ...), custom_call_target="tpu_custom_call" | custom-call | tf_op jit(solution)/shard_map/finish/pallas_call | solution.py:419
  (5 shorter events, 0.1 us)
Async XLA Ops:
  0.0 0.7 %copy-start.7 = (s32[1,2]{1,0:T(1,128)S(1)}, s32[1,2]{1,0:T(1,128)}, u32[]{:S(2)}) copy-start(s32[1,2]{1,0:T(1,128)} %param.10) | copy-start | bytes 28
  0.8 4.1 %copy-start.1 = (bf16[800,256]{1,0:T(8,128)(2,1)S(1)}, bf16[800,256]{1,0:T(8,128)(2,1)}, u32[]{:S(2)}) copy-start(bf16[800,256]{1,0:T(8,128)(2,1)} %constant.11.clone._.table_ref) | copy-start | bytes 1228804
  0.8 4.5 %collective-permute-start = (f32[1,128]{1,0:T(1,128)S(1)}, f32[1,128]{1,0:T(1,128)S(1)}, u32[]{:S(2)}, u32[]{:S(2)}) collective-permute-start(f32[1,128]{1,0:T(1,128)S(1)} %fusion), channel_id=1, source_target_pairs={{0,4},{4,0},{8,12},{12,8},{16,20},{20,16},{24,28},{28,24},{1,5},{5... | collective-permute-start | bytes 1544 | tf_op jit(solution)/shard_map/ppermute | solution.py:390
  3.8 1.1 %copy-start.5 = (s32[64]{0:T(128)S(1)}, s32[64]{0:T(128)}, u32[]{:S(2)}) copy-start(s32[64]{0:T(128)} %param.12) | copy-start | bytes 772
  3.8 1.1 %copy-start.6 = (s32[64]{0:T(128)S(1)}, s32[64]{0:T(128)}, u32[]{:S(2)}) copy-start(s32[64]{0:T(128)} %param.13) | copy-start | bytes 772
  4.8 8.9 %copy-start = (bf16[2,32,4096]{2,1,0:T(8,128)(2,1)S(1)}, bf16[2,32,4096]{2,1,0:T(8,128)(2,1)}, u32[]{:S(2)}) copy-start(bf16[2,32,4096]{2,1,0:T(8,128)(2,1)} %main_ref.1) | copy-start | bytes 1572868
  4.9 8.7 %collective-permute-start.3 = (bf16[2,16,4096]{2,1,0:T(8,128)(2,1)S(1)}, bf16[2,16,4096]{2,1,0:T(8,128)(2,1)S(1)}, u32[]{:S(2)}, u32[]{:S(2)}) collective-permute-start(bf16[2,16,4096]{2,1,0:T(8,128)(2,1)S(1)} %get-tuple-element.13), channel_id=1, source_target_pairs={{0,1},{1,2},{2,3},{3,0},{4,5},{5,6},{6,7},{7,4},{8,9},{9,10},{10,1... | collective-permute-start | bytes 786440 | tf_op jit(solution)/shard_map/ppermute | solution.py:385
  5.3 3.7 %collective-permute-start.1 = (f32[2,128]{1,0:T(2,128)S(1)}, f32[2,128]{1,0:T(2,128)S(1)}, u32[]{:S(2)}, u32[]{:S(2)}) collective-permute-start(f32[2,128]{1,0:T(2,128)S(1)} %pad_maximum_fusion.2), channel_id=1, source_target_pairs={{0,8},{4,12},{8,0},{12,4},{16,24},{20,28},{24,16},{28,20},{1,9},{5... | collective-permute-start | bytes 3080 | tf_op jit(solution)/shard_map/ppermute | solution.py:390
  7.4 6.3 %collective-permute-start.4 = (bf16[2,8,4096]{2,1,0:T(8,128)(2,1)S(1)}, bf16[2,8,4096]{2,1,0:T(8,128)(2,1)S(1)}, u32[]{:S(2)}, u32[]{:S(2)}) collective-permute-start(bf16[2,8,4096]{2,1,0:T(8,128)(2,1)S(1)} %get-tuple-element.14), channel_id=1, source_target_pairs={{0,3},{1,0},{2,1},{3,2},{4,7},{5,4},{6,5},{7,6},{8,11},{9,8},{10,9... | collective-permute-start | bytes 393224 | tf_op jit(solution)/shard_map/ppermute | solution.py:385
  9.0 4.7 %collective-permute-start.2 = (f32[4,128]{1,0:T(4,128)S(1)}, f32[4,128]{1,0:T(4,128)S(1)}, u32[]{:S(2)}, u32[]{:S(2)}) collective-permute-start(f32[4,128]{1,0:T(4,128)S(1)} %pad_maximum_fusion.1), channel_id=1, source_target_pairs={{0,16},{4,20},{8,24},{12,28},{16,0},{20,4},{24,8},{28,12},{1,17},{... | collective-permute-start | bytes 6152 | tf_op jit(solution)/shard_map/ppermute | solution.py:390
  13.7 1.9 %copy-start.2 = (bf16[384,352]{1,0:T(8,128)(2,1)S(1)}, bf16[384,352]{1,0:T(8,128)(2,1)}, u32[]{:S(2)}) copy-start(bf16[384,352]{1,0:T(8,128)(2,1)} %constant.12.clone.spread_rows_0) | copy-start | bytes 811012
  13.7 1.9 %copy-start.3 = (bf16[512,256]{1,0:T(8,128)(2,1)S(1)}, bf16[512,256]{1,0:T(8,128)(2,1)}, u32[]{:S(2)}) copy-start(bf16[512,256]{1,0:T(8,128)(2,1)} %constant.14.clone.spread_cols) | copy-start | bytes 786436
  13.7 1.9 %copy-start.4 = (bf16[64,192]{1,0:T(8,128)(2,1)S(1)}, bf16[64,192]{1,0:T(8,128)(2,1)}, u32[]{:S(2)}) copy-start(bf16[64,192]{1,0:T(8,128)(2,1)} %constant.13.clone.spread_rows_1) | copy-start | bytes 73732

commit v5 on v4

--- a/solution.py
+++ b/solution.py
@@ -53,13 +53,6 @@
     return np.concatenate(two_parts(full), axis=0)
 
 
-def row_spread(count):
-    _, real, imag = make_taps()
-    real, imag = band(real, count), band(imag, count)
-    taps = np.block([[real, -imag], [imag, real]])
-    return np.concatenate(two_parts(np.kron(taps, np.eye(ROWS))), axis=0)
-
-
 def column_band(taps):
     return np.kron(np.eye(2), np.pad(band(taps, HALF - 2 * REACH), ((0, 2 * REACH), (0, 0))).T)
 
@@ -112,14 +105,7 @@
     return both[:count] + both[count:] + product(high, matrix[half:])
 
 
-def row_product(matrix, value):
-    half = matrix.shape[0] // 2
-    high, low = split(value)
-    both = product(matrix, high)
-    return both[:half] + both[half:] + product(matrix[:half], low)
-
-
-def choose(plan, top_ref, bottom_ref, rows_ref, cols_ref, _, far_ref, near_ref, place_ref):
+def choose(plan, top_ref, bottom_ref, rows_ref, cols_ref, far_ref, near_ref, place_ref):
     find_places(plan, rows_ref, cols_ref, place_ref)
     first = lax.axis_index("beam") < lax.axis_size("beam") // 2
 
@@ -157,14 +143,17 @@
 def phases(
     plan,
     place_ref,
-    main_ref,
+    top_ref,
+    bottom_ref,
     far_ref,
     near_ref,
     table_ref,
+    beam_ref,
     cos_0,
     sin_0,
     cos_1,
     sin_1,
+    wave_out,
     strip_0,
     strip_1,
     patch_0,
@@ -173,22 +162,22 @@
     f32, bf16 = jnp.float32, jnp.bfloat16
     tiles = plan.grid_cols // LANES
     span = plan.span
-    strip_rows = main_ref.shape[1]
+    strip_rows = 2 * PAD
     strips, patches = (strip_0, strip_1), (patch_0, patch_1)
     first = lax.axis_index("beam") < lax.axis_size("beam") // 2
     far_at = jnp.where(first, 0, PAD + strip_rows)
     near_at = jnp.where(first, PAD + strip_rows, PAD - NEAR)
 
-    def widen(tile, carry):
-        lanes = pl.ds(pl.multiple_of(tile * LANES, LANES), LANES)
+    for tile in range(tiles):
+        lanes = slice(tile * LANES, (tile + 1) * LANES)
         at = tile * span
         for part in range(2):
+            strips[part][at + PAD : at + 2 * PAD, :] = top_ref[part, :, lanes].astype(f32)
+            strips[part][at + 2 * PAD : at + 3 * PAD, :] = bottom_ref[part, :, lanes].astype(f32)
             strips[part][pl.ds(at + far_at, PAD), :] = far_ref[part, :, lanes].astype(f32)
-            strips[part][pl.ds(at + PAD, strip_rows), :] = main_ref[part, :, lanes].astype(f32)
             strips[part][pl.ds(at + near_at, NEAR), :] = near_ref[part, :, lanes].astype(f32)
-        return carry
-
-    lax.fori_loop(0, tiles, widen, 0, unroll=4)
+
+    wave_out[...] = common_wave(plan, beam_ref, None)
     lane = lax.broadcasted_iota(jnp.int32, (1, LANES), 1)
     cos_fit = fit(lambda t: np.cos(np.sqrt(t)), MIDDLE**2, 4)
     sin_fit = fit(lambda t: np.sinc(np.sqrt(t) / np.pi), MIDDLE**2, 4)
@@ -229,46 +218,59 @@
             sin_out[group * size : (group + 2) * size] = phase * horner(sin_fit, square)
 
 
-def common_wave(plan, beam_ref, wave_ref):
+def common_wave(plan, beam_ref, total):
     f32 = jnp.float32
-    count = wave_ref.shape[1] // ROWS
-    shape = (-(-count // ROWS) * ROWS, LANES)
     turn_fit = fit(lambda t: 2 * np.pi * np.sinc(2 * np.sqrt(t)), 0.0625, 5)
     first_row, first_col = plan.origin()
+    shape = plan.wave_shape
     dx = lax.broadcasted_iota(jnp.int32, shape, 0) + (first_row - 2 * REACH)
     lane = lax.broadcasted_iota(jnp.int32, shape, 1)
-    upper = lane >= HALF
     dy = (lane & (HALF - 1)) + (first_col - 2 * REACH)
     dx = dx.astype(f32) * (1.0 / plan.grid_rows)
     dy = dy.astype(f32) * (1.0 / plan.grid_cols)
-    quarter = jnp.where(upper, 0.25, 0.0).astype(f32)
-
-    numbers = [
-        jnp.broadcast_to(beam_ref[:, i : i + 1], (plan.beams, LANES)) for i in range(NUMBERS)
-    ]
-    both = jnp.zeros(shape, f32)
-    for beam in range(plan.beams):
+    quarter = jnp.where(lane >= HALF, 0.25, 0.0).astype(f32)
+    beams = beam_ref.shape[0]
+    numbers = [jnp.broadcast_to(beam_ref[:, i : i + 1], (beams, LANES)) for i in range(NUMBERS)]
+    for beam in range(beams):
         row, col, weight = [number[beam : beam + 1] for number in numbers]
         turns = row * dx + (col * dy - quarter)
         left = 0.25 - jnp.abs(turns - jnp.round(turns))
-        both = both + (weight * left) * horner(turn_fit, left * left)
+        term = (weight * left) * horner(turn_fit, left * left)
+        total = term if total is None else total + term
+    return total
+
+
+def expand_wave(both, wave_ref):
+    upper = lax.broadcasted_iota(jnp.int32, both.shape, 1) >= HALF
     turned = pltpu.roll(both, HALF, 1)
     real = jnp.where(upper, turned, both)
     imag = jnp.where(upper, both, turned)
-    for r in range(count):
+    for r in range(wave_ref.shape[1] // ROWS):
         at = slice(r * ROWS, (r + 1) * ROWS)
         wave_ref[0, at, :] = jnp.broadcast_to(real[r : r + 1], (ROWS, LANES))
         wave_ref[1, at, :] = jnp.broadcast_to(imag[r : r + 1], (ROWS, LANES))
 
 
-def propagate(waves, row_matrix, column_matrix):
-    rows = []
-    for i in range(0, len(waves), 2):
-        both = row_product(row_matrix[...], jnp.concatenate(waves[i : i + 2], axis=1))
-        half = both.shape[0] // 2
-        for lanes in (slice(0, LANES), slice(LANES, 2 * LANES)):
-            rows.append(jnp.concatenate([both[:half, lanes], both[half:, lanes]], axis=1))
-    return column_product(jnp.concatenate(rows, axis=0), column_matrix[...])
+def spread_rows(wave, count):
+    _, real_taps, imag_taps = make_taps()
+    half = wave.shape[0] // 2
+    out = []
+    for at in range(count):
+        sums = []
+        for base in (0, half):
+            rows = [
+                wave[base + (at + j) * ROWS : base + (at + j + 1) * ROWS] for j in range(2 * REACH + 1)
+            ]
+            pairs = [rows[REACH]] + [rows[REACH - j] + rows[REACH + j] for j in range(1, REACH + 1)]
+            sums.append(
+                [
+                    sum(float(taps[REACH + j]) * pairs[j] for j in range(start, REACH + 1))
+                    for taps, start in ((real_taps, 0), (imag_taps, 1))
+                ]
+            )
+        (real_real, real_imag), (imag_real, imag_imag) = sums
+        out.append(jnp.concatenate([real_real - imag_imag, imag_real + real_imag], axis=1))
+    return jnp.concatenate(out, axis=0)
 
 
 def turn(real, imag, cos, sin):
@@ -284,6 +286,7 @@
         self.take_rows = pixels // self.take_cols
         self.halo = [3 * REACH, 2 * REACH]
         self.span = span
+        self.wave_shape = (-(-(self.take_rows + 4 * REACH) // ROWS) * ROWS, LANES)
         self.phase_rows = [self.take_rows + 4 * REACH, self.take_rows + 2 * REACH]
         self.stored = [-(-(count + 2 * REACH) // ROWS) * ROWS for count in self.phase_rows]
 
@@ -295,29 +298,30 @@
 def finish(
     plan,
     beam_ref,
+    half_wave,
     cos_0,
     sin_0,
     cos_1,
     sin_1,
-    spread_rows_0,
-    spread_rows_1,
     spread_cols,
     out_ref,
     start,
 ):
-    common_wave(plan, beam_ref, start)
+    expand_wave(common_wave(plan, beam_ref, half_wave[...]), start)
     count = plan.phase_rows[0] * ROWS
     waves = []
     for group in range(plan.groups):
         at = slice(group * count, (group + 1) * count)
         waves.append(turn(start[0], start[1], cos_0[at], sin_0[at]))
-    wave = propagate(waves, spread_rows_0, spread_cols)
+    rows = [spread_rows(wave, plan.phase_rows[1]) for wave in waves]
+    wave = column_product(jnp.concatenate(rows, axis=0), spread_cols[...])
     count = plan.phase_rows[1] * ROWS
     waves = []
     for group in range(plan.groups):
         at = slice(group * count, (group + 1) * count)
         waves.append(turn(wave[at, :LANES], wave[at, LANES:], cos_1[at], sin_1[at]))
-    wave = propagate(waves, spread_rows_1, spread_cols)
+    rows = [spread_rows(wave, plan.take_rows) for wave in waves]
+    wave = column_product(jnp.concatenate(rows, axis=0), spread_cols[...])
     lane = lax.broadcasted_iota(jnp.int32, (ROWS, LANES), 1)
     blocks = []
     count = plan.take_rows * ROWS
@@ -370,11 +374,11 @@
             jax.ShapeDtypeStruct((slices, NEAR, grid_cols), bf16),
             jax.ShapeDtypeStruct((8, plan.probes), jnp.int32),
         ],
-        in_specs=[vmem] * 5,
+        in_specs=[vmem] * 4,
         out_specs=[vmem] * 3,
         compiler_params=pltpu.CompilerParams(vmem_limit_bytes=2 << 20),
         name="choose",
-    )(top, bottom, probe_rows[None], probe_cols[None], table)
+    )(top, bottom, probe_rows[None], probe_cols[None])
 
     def pass_on(rows, step):
         pairs = []
@@ -386,9 +390,11 @@
 
     far = pass_on(far, 1)
     near = pass_on(near, -1)
+    other = None
     for reach in ROUNDS(beam_parts):
+        if other is not None:
+            known = jnp.concatenate([known, other], axis=0)
         other = lax.ppermute(known, "beam", [(i, i ^ reach) for i in range(beam_parts)])
-        known = jnp.concatenate([known, other], axis=0)
 
     shapes = [(plan.groups * count * ROWS, LANES) for count in plan.phase_rows]
     shapes = [jax.ShapeDtypeStruct(shape, f32) for shape in shapes]
@@ -398,25 +404,26 @@
         patches.append(pltpu.VMEM((plan.probes // 2 * stored, LANES), kind))
     call = pl.pallas_call(
         functools.partial(phases, plan),
-        out_shape=[shapes[0], shapes[0], shapes[1], shapes[1]],
-        in_specs=[smem] + [vmem] * 4,
-        out_specs=[vmem] * 4,
+        out_shape=[shapes[0]] * 2 + [shapes[1]] * 2 + [jax.ShapeDtypeStruct(plan.wave_shape, f32)],
+        in_specs=[smem] + [vmem] * 6,
+        out_specs=[vmem] * 5,
         scratch_shapes=[pltpu.VMEM((tiles * plan.span, LANES), f32)] * 2 + patches,
         compiler_params=params,
         name="phases",
     )
-    cos_0, sin_0, cos_1, sin_1 = call(places, atom_counts, far, near, table)
+    cos_0, sin_0, cos_1, sin_1, wave = call(
+        places, top, bottom, far, near, table, known
+    )
     call = pl.pallas_call(
         functools.partial(finish, plan),
         out_shape=jax.ShapeDtypeStruct((plan.pixels, plan.probes), f32),
-        in_specs=[vmem] * 8,
+        in_specs=[vmem] * 7,
         out_specs=vmem,
         scratch_shapes=[pltpu.VMEM((2, plan.phase_rows[0] * ROWS, LANES), f32)],
         compiler_params=params,
         name="finish",
     )
-    tables = [row_spread(plan.phase_rows[1]), row_spread(plan.take_rows), column_spread()]
-    out = call(known, cos_0, sin_0, cos_1, sin_1, *[jnp.asarray(table) for table in tables])
+    out = call(other, wave, cos_0, sin_0, cos_1, sin_1, jnp.asarray(column_spread()))
     return out.T
 
 

time: 18.1 us -> 18.1 us (level)
  starting transfers between devices: 8.97 us -> 10.7 us
  waiting for transfers between devices: 2.71 us -> 1.65 us
  Pallas kernels: 4.19 us -> 3.64 us
    ppermute x2, starting transfers between devices: 0.76 us -> 2 us  [pass_on(): return lax.ppermute(rows, ('beam', 'tile'), pairs)]
    ppermute x3, waiting for transfers between devices: 2.7 us -> 1.64 us  [window(): lax.ppermute(known, 'beam', [(i, i ^ reach) for i in range(beam_parts)])]
    pallas_call x2, Pallas kernels: 4.14 us -> 3.59 us  [the longest x1 1.8 us: window(): call(other, wave, cos_0, sin_0, cos_1, sin_1, jnp.asarray(column_spread()))]
    ppermute x3, starting transfers between devices: 8.21 us -> 8.66 us  [window(): lax.ppermute(known, 'beam', [(i, i ^ reach) for i in range(beam_parts)])]
  transfers between devices with their start and end apart: 5 -> 5, of which waited for: 3 -> 2; matrix products, arithmetic and copies ran while one was open for 6% -> 1% of each run, Pallas kernels for 0% -> 10%
where the time goes in v5:
time: 18.1 us; the launch traced here: 17.9 us
  starting transfers between devices  10.7 us (59%)
  Pallas kernels  3.64 us (20%)
  waiting for transfers between devices  1.65 us (9%)
  local copies, waits for them, and re-layouts  1.12 us (6%)
  between operations  0.75 us (4%)
    ppermute x3, starting transfers between devices, window(): lax.ppermute(known, 'beam', [(i, i ^ reach) for i in range(beam_parts)])  8.66 us
    ppermute x2, starting transfers between devices, pass_on(): return lax.ppermute(rows, ('beam', 'tile'), pairs)  2 us
    pallas_call x1, Pallas kernels, window(): call(other, wave, cos_0, sin_0, cos_1, sin_1, jnp.asarray(column_spread()))  1.8 us
    pallas_call x1, Pallas kernels, window(): call(places, top, bottom, far, near, table, known)  1.79 us
    ppermute x3, waiting for transfers between devices, window(): lax.ppermute(known, 'beam', [(i, i ^ reach) for i in range(beam_parts)])  1.64 us
    slice x1, local copies, waits for them, and re-layouts, window(): top, bottom = (atom_counts[:, :PAD], atom_counts[:, strip_rows - PAD:])  1.09 us
  transfers between devices with their start and end apart: 5, of which 2 were waited for; matrix products, arithmetic and copies ran while one was open for 1% of the time, Pallas kernels for 10%

profile of v5, /device:TPU:0, one launch (start us, length us, event | category | flops | bytes accessed | tf_op | source)
XLA Modules:
  0.0 17.9 jit_solution(2280297099679145873)
XLA Ops:
  0.0 0.0 copy-start.2
  0.0 0.0 copy-start.3
  0.0 1.1 %fusion.1 = (bf16[2,16,4096]{2,1,0:T(8,128)(2,1)S(1)}, bf16[2,16,4096]{2,1,0:T(8,128)(2,1)S(1)}) fusion(bf16[2,32,4096]{2,1,0:T(8,128)(2,1)} %param.7), kind=kLoop, calls=%fused_computation.5 | loop fusion | bytes 1048576 | tf_op jit(solution)/shard_map/slice | solution.py:363
  1.1 0.0 copy-start
  1.1 0.0 copy-done.2
  1.1 0.0 copy-done.3
  1.2 0.0 copy-start.4
  1.2 0.5 %collective-permute-start.3 = (bf16[2,16,4096]{2,1,0:T(8,128)(2,1)S(1)}, bf16[2,16,4096]{2,1,0:T(8,128)(2,1)S(1)}, u32[]{:S(2)}, u32[]{:S(2)}) collective-permute-start(bf16[2,16,4096]{2,1,0:T(8,128)(2,1)S(1)} %get-tuple-element.14), channel_id=1, source_target_pairs={{0,1},{1,2},{2,3},{3,0},{4,5},{5,6},{6,7},{7,4},{8,9},{9,10},{10,1... | collective-permute-start | bytes 786440 | tf_op jit(solution)/shard_map/ppermute | solution.py:389
  2.4 0.0 copy-done.4
  2.4 0.1 fusion
  2.5 2.5 %collective-permute-start = (f32[1,128]{1,0:T(1,128)S(1)}, f32[1,128]{1,0:T(1,128)S(1)}, u32[]{:S(2)}, u32[]{:S(2)}) collective-permute-start(f32[1,128]{1,0:T(1,128)S(1)} %fusion), channel_id=1, source_target_pairs={{0,4},{4,0},{8,12},{12,8},{16,20},{20,16},{24,28},{28,24},{1,5},{5... | collective-permute-start | bytes 1544 | tf_op jit(solution)/shard_map/ppermute | solution.py:397
  5.0 1.5 %collective-permute-start.4 = (bf16[2,8,4096]{2,1,0:T(8,128)(2,1)S(1)}, bf16[2,8,4096]{2,1,0:T(8,128)(2,1)S(1)}, u32[]{:S(2)}, u32[]{:S(2)}) collective-permute-start(bf16[2,8,4096]{2,1,0:T(8,128)(2,1)S(1)} %get-tuple-element.15), channel_id=1, source_target_pairs={{0,3},{1,0},{2,1},{3,2},{4,7},{5,4},{6,5},{7,6},{8,11},{9,8},{10,9... | collective-permute-start | bytes 393224 | tf_op jit(solution)/shard_map/ppermute | solution.py:389
  6.4 0.1 collective-permute-done
  6.5 2.1 %collective-permute-start.1 = (f32[2,128]{1,0:T(2,128)S(1)}, f32[2,128]{1,0:T(2,128)S(1)}, u32[]{:S(2)}, u32[]{:S(2)}) collective-permute-start(f32[2,128]{1,0:T(2,128)S(1)} %pad_maximum_fusion.1), channel_id=1, source_target_pairs={{0,8},{4,12},{8,0},{12,4},{16,24},{20,28},{24,16},{28,20},{1,9},{5... | collective-permute-start | bytes 3080 | tf_op jit(solution)/shard_map/ppermute | solution.py:397
  8.6 1.6 %collective-permute-done.1 = f32[2,128]{1,0:T(2,128)S(1)} collective-permute-done((f32[2,128]{1,0:T(2,128)S(1)}, f32[2,128]{1,0:T(2,128)S(1)}, u32[]{:S(2)}, u32[]{:S(2)}) %collective-permute-start.1) | collective-permute-done | bytes 1056 | tf_op jit(solution)/shard_map/ppermute | solution.py:397
  10.2 4.1 %collective-permute-start.2 = (f32[4,128]{1,0:T(4,128)S(1)}, f32[4,128]{1,0:T(4,128)S(1)}, u32[]{:S(2)}, u32[]{:S(2)}) collective-permute-start(f32[4,128]{1,0:T(4,128)S(1)} %pad_maximum_fusion.beam_ref), channel_id=1, source_target_pairs={{0,16},{4,20},{8,24},{12,28},{16,0},{20,4},{24,8},{28,12},{1,17},{... | collective-permute-start | bytes 6152 | tf_op jit(solution)/shard_map/ppermute | solution.py:397
  14.3 0.0 collective-permute-done.4.near_ref
  14.3 0.0 collective-permute-done.3.far_ref
  14.3 0.0 copy-done
  14.3 0.0 copy-start.1
  14.3 1.8 %phases.1 = (f32[704,128]{1,0:T(8,128)S(1)}, f32[704,128]{1,0:T(8,128)S(1)}, f32[384,128]{1,0:T(8,128)S(1)}, f32[384,128]{1,0:T(8,128)S(1)}, f32[24,128]{1,0:T(8,128)S(1)}) custom-call(s32[8,64]{1,0:T(8,128)S(1)} %get-tuple-element.13.place_ref, bf16[2,16,4096]{2,1,0:T(8,128)(2,1)S(1)} %get-tuple-element.22.top_ref, ...), custom_call_target="tpu_custom_call" | custom-call | tf_op jit(solution)/shard_map/phases/pallas_call | solution.py:414
  16.1 0.0 collective-permute-done.2.beam_ref
  16.1 0.0 copy-done.1
  16.1 1.8 %finish.1 = f32[32,64]{1,0:T(8,128)} custom-call(f32[4,128]{1,0:T(4,128)S(1)} %collective-permute-done.2.beam_ref, f32[24,128]{1,0:T(8,128)S(1)} %get-tuple-element.16.half_wave, f32[704,128]{1,0:T(8,128)S(1)} %get-tuple-element.17.cos_0, f32[704,128]{1,0:T(8,128)S(1)} %get-tuple-element.18.sin_0, f32[384,128]{1,0:T(8,128)S(1)} %get-tuple-element.19.cos_1, ...), custom_call_target="tpu_custom_call" | custom-call | tf_op jit(solution)/shard_map/finish/pallas_call | solution.py:426
  (4 shorter events, 0.1 us)
Async XLA Ops:
  0.0 1.1 %copy-start.2 = (s32[64]{0:T(128)S(1)}, s32[64]{0:T(128)}, u32[]{:S(2)}) copy-start(s32[64]{0:T(128)} %param.10) | copy-start | bytes 772
  0.0 1.1 %copy-start.3 = (s32[64]{0:T(128)S(1)}, s32[64]{0:T(128)}, u32[]{:S(2)}) copy-start(s32[64]{0:T(128)} %param.11) | copy-start | bytes 772
  1.1 13.2 %copy-start = (bf16[800,256]{1,0:T(8,128)(2,1)S(1)}, bf16[800,256]{1,0:T(8,128)(2,1)}, u32[]{:S(2)}) copy-start(bf16[800,256]{1,0:T(8,128)(2,1)} %constant.7.clone.table_ref) | copy-start | bytes 1228804
  1.2 1.2 %copy-start.4 = (s32[1,2]{1,0:T(1,128)S(1)}, s32[1,2]{1,0:T(1,128)}, u32[]{:S(2)}) copy-start(s32[1,2]{1,0:T(1,128)} %param.8) | copy-start | bytes 28
  1.2 13.1 %collective-permute-start.3 = (bf16[2,16,4096]{2,1,0:T(8,128)(2,1)S(1)}, bf16[2,16,4096]{2,1,0:T(8,128)(2,1)S(1)}, u32[]{:S(2)}, u32[]{:S(2)}) collective-permute-start(bf16[2,16,4096]{2,1,0:T(8,128)(2,1)S(1)} %get-tuple-element.14), channel_id=1, source_target_pairs={{0,1},{1,2},{2,3},{3,0},{4,5},{5,6},{6,7},{7,4},{8,9},{9,10},{10,1... | collective-permute-start | bytes 786440 | tf_op jit(solution)/shard_map/ppermute | solution.py:389
  2.5 4.0 %collective-permute-start = (f32[1,128]{1,0:T(1,128)S(1)}, f32[1,128]{1,0:T(1,128)S(1)}, u32[]{:S(2)}, u32[]{:S(2)}) collective-permute-start(f32[1,128]{1,0:T(1,128)S(1)} %fusion), channel_id=1, source_target_pairs={{0,4},{4,0},{8,12},{12,8},{16,20},{20,16},{24,28},{28,24},{1,5},{5... | collective-permute-start | bytes 1544 | tf_op jit(solution)/shard_map/ppermute | solution.py:397
  5.0 9.3 %collective-permute-start.4 = (bf16[2,8,4096]{2,1,0:T(8,128)(2,1)S(1)}, bf16[2,8,4096]{2,1,0:T(8,128)(2,1)S(1)}, u32[]{:S(2)}, u32[]{:S(2)}) collective-permute-start(bf16[2,8,4096]{2,1,0:T(8,128)(2,1)S(1)} %get-tuple-element.15), channel_id=1, source_target_pairs={{0,3},{1,0},{2,1},{3,2},{4,7},{5,4},{6,5},{7,6},{8,11},{9,8},{10,9... | collective-permute-start | bytes 393224 | tf_op jit(solution)/shard_map/ppermute | solution.py:389
  6.5 3.7 %collective-permute-start.1 = (f32[2,128]{1,0:T(2,128)S(1)}, f32[2,128]{1,0:T(2,128)S(1)}, u32[]{:S(2)}, u32[]{:S(2)}) collective-permute-start(f32[2,128]{1,0:T(2,128)S(1)} %pad_maximum_fusion.1), channel_id=1, source_target_pairs={{0,8},{4,12},{8,0},{12,4},{16,24},{20,28},{24,16},{28,20},{1,9},{5... | collective-permute-start | bytes 3080 | tf_op jit(solution)/shard_map/ppermute | solution.py:397
  10.2 5.9 %collective-permute-start.2 = (f32[4,128]{1,0:T(4,128)S(1)}, f32[4,128]{1,0:T(4,128)S(1)}, u32[]{:S(2)}, u32[]{:S(2)}) collective-permute-start(f32[4,128]{1,0:T(4,128)S(1)} %pad_maximum_fusion.beam_ref), channel_id=1, source_target_pairs={{0,16},{4,20},{8,24},{12,28},{16,0},{20,4},{24,8},{28,12},{1,17},{... | collective-permute-start | bytes 6152 | tf_op jit(solution)/shard_map/ppermute | solution.py:397
  14.3 1.8 %copy-start.1 = (bf16[512,256]{1,0:T(8,128)(2,1)S(1)}, bf16[512,256]{1,0:T(8,128)(2,1)}, u32[]{:S(2)}) copy-start(bf16[512,256]{1,0:T(8,128)(2,1)} %constant.8.clone.spread_cols) | copy-start | bytes 786436

commit v6 on v5

--- a/solution.py
+++ b/solution.py
@@ -142,7 +142,7 @@
 
 def phases(
     plan,
-    place_ref,
+    found_ref,
     top_ref,
     bottom_ref,
     far_ref,
@@ -158,12 +158,16 @@
     strip_1,
     patch_0,
     patch_1,
+    place_ref,
+    arrived,
 ):
     f32, bf16 = jnp.float32, jnp.bfloat16
     tiles = plan.grid_cols // LANES
     span = plan.span
     strip_rows = 2 * PAD
     strips, patches = (strip_0, strip_1), (patch_0, patch_1)
+    transfer = pltpu.make_async_copy(found_ref, place_ref, arrived)
+    transfer.start()
     first = lax.axis_index("beam") < lax.axis_size("beam") // 2
     far_at = jnp.where(first, 0, PAD + strip_rows)
     near_at = jnp.where(first, PAD + strip_rows, PAD - NEAR)
@@ -178,7 +182,10 @@
             strips[part][pl.ds(at + near_at, NEAR), :] = near_ref[part, :, lanes].astype(f32)
 
     wave_out[...] = common_wave(plan, beam_ref, None)
+    transfer.wait()
     lane = lax.broadcasted_iota(jnp.int32, (1, LANES), 1)
+    lower = jnp.where(lane < HALF, 1.0, 0.0).astype(bf16)
+    upper = jnp.where(lane < HALF, 0.0, 1.0).astype(bf16)
     cos_fit = fit(lambda t: np.cos(np.sqrt(t)), MIDDLE**2, 4)
     sin_fit = fit(lambda t: np.sinc(np.sqrt(t) / np.pi), MIDDLE**2, 4)
     outs = ((cos_0, sin_0), (cos_1, sin_1))
@@ -199,7 +206,7 @@
 
         for pair in range(plan.probes // 2):
             probe = pair // ROWS * 2 * ROWS + pair % ROWS
-            both = jnp.where(lane < HALF, window(probe), window(probe + ROWS))
+            both = lower * window(probe).astype(bf16) + upper * window(probe + ROWS).astype(bf16)
             patch[pair * stored : (pair + 1) * stored, :] = both.astype(patch.dtype)
 
         count = ROWS * stored
@@ -405,9 +412,11 @@
     call = pl.pallas_call(
         functools.partial(phases, plan),
         out_shape=[shapes[0]] * 2 + [shapes[1]] * 2 + [jax.ShapeDtypeStruct(plan.wave_shape, f32)],
-        in_specs=[smem] + [vmem] * 6,
+        in_specs=[vmem] * 7,
         out_specs=[vmem] * 5,
-        scratch_shapes=[pltpu.VMEM((tiles * plan.span, LANES), f32)] * 2 + patches,
+        scratch_shapes=[pltpu.VMEM((tiles * plan.span, LANES), f32)] * 2
+        + patches
+        + [pltpu.SMEM((8, plan.probes), jnp.int32), pltpu.SemaphoreType.DMA],
         compiler_params=params,
         name="phases",
     )

time: 18.1 us -> 17.9 us (0.989)
  transfers between devices with their start and end apart: 5 -> 5, of which waited for: 2 -> 2; matrix products, arithmetic and copies ran while one was open for 1% -> 1% of each run, Pallas kernels for 10% -> 9%
where the time goes in v6:
time: 17.9 us; the launch traced here: 17.8 us
  starting transfers between devices  10.7 us (60%)
  Pallas kernels  3.52 us (20%)
  waiting for transfers between devices  1.65 us (9%)
  local copies, waits for them, and re-layouts  1.12 us (6%)
  between operations  0.75 us (4%)
    ppermute x3, starting transfers between devices, window(): lax.ppermute(known, 'beam', [(i, i ^ reach) for i in range(beam_parts)])  8.66 us
    ppermute x2, starting transfers between devices, pass_on(): return lax.ppermute(rows, ('beam', 'tile'), pairs)  2 us
    pallas_call x1, Pallas kernels, window(): call(other, wave, cos_0, sin_0, cos_1, sin_1, jnp.asarray(column_spread()))  1.8 us
    pallas_call x1, Pallas kernels, window(): call(places, top, bottom, far, near, table, known)  1.68 us
    ppermute x3, waiting for transfers between devices, window(): lax.ppermute(known, 'beam', [(i, i ^ reach) for i in range(beam_parts)])  1.64 us
    slice x1, local copies, waits for them, and re-layouts, window(): top, bottom = (atom_counts[:, :PAD], atom_counts[:, strip_rows - PAD:])  1.09 us
  transfers between devices with their start and end apart: 5, of which 2 were waited for; matrix products, arithmetic and copies ran while one was open for 1% of the time, Pallas kernels for 9%

profile of v6, /device:TPU:0, one launch (start us, length us, event | category | flops | bytes accessed | tf_op | source)
XLA Modules:
  0.0 17.8 jit_solution(8559402424435550571)
XLA Ops:
  0.0 0.0 copy-start.2
  0.0 0.0 copy-start.3
  0.0 1.1 %fusion.1 = (bf16[2,16,4096]{2,1,0:T(8,128)(2,1)S(1)}, bf16[2,16,4096]{2,1,0:T(8,128)(2,1)S(1)}) fusion(bf16[2,32,4096]{2,1,0:T(8,128)(2,1)} %param.7), kind=kLoop, calls=%fused_computation.5 | loop fusion | bytes 1048576 | tf_op jit(solution)/shard_map/slice | solution.py:370
  1.1 0.0 copy-start
  1.1 0.0 copy-done.2
  1.1 0.0 copy-done.3
  1.2 0.0 copy-start.4
  1.2 0.5 %collective-permute-start.3 = (bf16[2,16,4096]{2,1,0:T(8,128)(2,1)S(1)}, bf16[2,16,4096]{2,1,0:T(8,128)(2,1)S(1)}, u32[]{:S(2)}, u32[]{:S(2)}) collective-permute-start(bf16[2,16,4096]{2,1,0:T(8,128)(2,1)S(1)} %get-tuple-element.14), channel_id=1, source_target_pairs={{0,1},{1,2},{2,3},{3,0},{4,5},{5,6},{6,7},{7,4},{8,9},{9,10},{10,1... | collective-permute-start | bytes 786440 | tf_op jit(solution)/shard_map/ppermute | solution.py:396
  2.4 0.0 copy-done.4
  2.4 0.1 fusion
  2.5 2.5 %collective-permute-start = (f32[1,128]{1,0:T(1,128)S(1)}, f32[1,128]{1,0:T(1,128)S(1)}, u32[]{:S(2)}, u32[]{:S(2)}) collective-permute-start(f32[1,128]{1,0:T(1,128)S(1)} %fusion), channel_id=1, source_target_pairs={{0,4},{4,0},{8,12},{12,8},{16,20},{20,16},{24,28},{28,24},{1,5},{5... | collective-permute-start | bytes 1544 | tf_op jit(solution)/shard_map/ppermute | solution.py:404
  5.0 1.5 %collective-permute-start.4 = (bf16[2,8,4096]{2,1,0:T(8,128)(2,1)S(1)}, bf16[2,8,4096]{2,1,0:T(8,128)(2,1)S(1)}, u32[]{:S(2)}, u32[]{:S(2)}) collective-permute-start(bf16[2,8,4096]{2,1,0:T(8,128)(2,1)S(1)} %get-tuple-element.15), channel_id=1, source_target_pairs={{0,3},{1,0},{2,1},{3,2},{4,7},{5,4},{6,5},{7,6},{8,11},{9,8},{10,9... | collective-permute-start | bytes 393224 | tf_op jit(solution)/shard_map/ppermute | solution.py:396
  6.4 0.1 collective-permute-done
  6.5 2.1 %collective-permute-start.1 = (f32[2,128]{1,0:T(2,128)S(1)}, f32[2,128]{1,0:T(2,128)S(1)}, u32[]{:S(2)}, u32[]{:S(2)}) collective-permute-start(f32[2,128]{1,0:T(2,128)S(1)} %pad_maximum_fusion.1), channel_id=1, source_target_pairs={{0,8},{4,12},{8,0},{12,4},{16,24},{20,28},{24,16},{28,20},{1,9},{5... | collective-permute-start | bytes 3080 | tf_op jit(solution)/shard_map/ppermute | solution.py:404
  8.6 1.6 %collective-permute-done.1 = f32[2,128]{1,0:T(2,128)S(1)} collective-permute-done((f32[2,128]{1,0:T(2,128)S(1)}, f32[2,128]{1,0:T(2,128)S(1)}, u32[]{:S(2)}, u32[]{:S(2)}) %collective-permute-start.1) | collective-permute-done | bytes 1056 | tf_op jit(solution)/shard_map/ppermute | solution.py:404
  10.2 4.1 %collective-permute-start.2 = (f32[4,128]{1,0:T(4,128)S(1)}, f32[4,128]{1,0:T(4,128)S(1)}, u32[]{:S(2)}, u32[]{:S(2)}) collective-permute-start(f32[4,128]{1,0:T(4,128)S(1)} %pad_maximum_fusion.beam_ref), channel_id=1, source_target_pairs={{0,16},{4,20},{8,24},{12,28},{16,0},{20,4},{24,8},{28,12},{1,17},{... | collective-permute-start | bytes 6152 | tf_op jit(solution)/shard_map/ppermute | solution.py:404
  14.3 0.0 collective-permute-done.4.near_ref
  14.3 0.0 collective-permute-done.3.far_ref
  14.3 0.0 copy-done
  14.3 0.0 copy-start.1
  14.3 1.7 %phases.1 = (f32[704,128]{1,0:T(8,128)S(1)}, f32[704,128]{1,0:T(8,128)S(1)}, f32[384,128]{1,0:T(8,128)S(1)}, f32[384,128]{1,0:T(8,128)S(1)}, f32[24,128]{1,0:T(8,128)S(1)}) custom-call(s32[8,64]{1,0:T(8,128)S(1)} %get-tuple-element.13.found_ref, bf16[2,16,4096]{2,1,0:T(8,128)(2,1)S(1)} %get-tuple-element.22.top_ref, ...), custom_call_target="tpu_custom_call" | custom-call | tf_op jit(solution)/shard_map/phases/pallas_call | solution.py:423
  16.0 0.0 collective-permute-done.2.beam_ref
  16.0 0.0 copy-done.1
  16.0 1.8 %finish.1 = f32[32,64]{1,0:T(8,128)} custom-call(f32[4,128]{1,0:T(4,128)S(1)} %collective-permute-done.2.beam_ref, f32[24,128]{1,0:T(8,128)S(1)} %get-tuple-element.16.half_wave, f32[704,128]{1,0:T(8,128)S(1)} %get-tuple-element.17.cos_0, f32[704,128]{1,0:T(8,128)S(1)} %get-tuple-element.18.sin_0, f32[384,128]{1,0:T(8,128)S(1)} %get-tuple-element.19.cos_1, ...), custom_call_target="tpu_custom_call" | custom-call | tf_op jit(solution)/shard_map/finish/pallas_call | solution.py:435
  (4 shorter events, 0.1 us)
Async XLA Ops:
  0.0 1.1 %copy-start.2 = (s32[64]{0:T(128)S(1)}, s32[64]{0:T(128)}, u32[]{:S(2)}) copy-start(s32[64]{0:T(128)} %param.10) | copy-start | bytes 772
  0.0 1.1 %copy-start.3 = (s32[64]{0:T(128)S(1)}, s32[64]{0:T(128)}, u32[]{:S(2)}) copy-start(s32[64]{0:T(128)} %param.11) | copy-start | bytes 772
  1.1 13.2 %copy-start = (bf16[800,256]{1,0:T(8,128)(2,1)S(1)}, bf16[800,256]{1,0:T(8,128)(2,1)}, u32[]{:S(2)}) copy-start(bf16[800,256]{1,0:T(8,128)(2,1)} %constant.7.clone.table_ref) | copy-start | bytes 1228804
  1.2 1.2 %copy-start.4 = (s32[1,2]{1,0:T(1,128)S(1)}, s32[1,2]{1,0:T(1,128)}, u32[]{:S(2)}) copy-start(s32[1,2]{1,0:T(1,128)} %param.8) | copy-start | bytes 28
  1.2 13.1 %collective-permute-start.3 = (bf16[2,16,4096]{2,1,0:T(8,128)(2,1)S(1)}, bf16[2,16,4096]{2,1,0:T(8,128)(2,1)S(1)}, u32[]{:S(2)}, u32[]{:S(2)}) collective-permute-start(bf16[2,16,4096]{2,1,0:T(8,128)(2,1)S(1)} %get-tuple-element.14), channel_id=1, source_target_pairs={{0,1},{1,2},{2,3},{3,0},{4,5},{5,6},{6,7},{7,4},{8,9},{9,10},{10,1... | collective-permute-start | bytes 786440 | tf_op jit(solution)/shard_map/ppermute | solution.py:396
  2.5 4.0 %collective-permute-start = (f32[1,128]{1,0:T(1,128)S(1)}, f32[1,128]{1,0:T(1,128)S(1)}, u32[]{:S(2)}, u32[]{:S(2)}) collective-permute-start(f32[1,128]{1,0:T(1,128)S(1)} %fusion), channel_id=1, source_target_pairs={{0,4},{4,0},{8,12},{12,8},{16,20},{20,16},{24,28},{28,24},{1,5},{5... | collective-permute-start | bytes 1544 | tf_op jit(solution)/shard_map/ppermute | solution.py:404
  5.0 9.3 %collective-permute-start.4 = (bf16[2,8,4096]{2,1,0:T(8,128)(2,1)S(1)}, bf16[2,8,4096]{2,1,0:T(8,128)(2,1)S(1)}, u32[]{:S(2)}, u32[]{:S(2)}) collective-permute-start(bf16[2,8,4096]{2,1,0:T(8,128)(2,1)S(1)} %get-tuple-element.15), channel_id=1, source_target_pairs={{0,3},{1,0},{2,1},{3,2},{4,7},{5,4},{6,5},{7,6},{8,11},{9,8},{10,9... | collective-permute-start | bytes 393224 | tf_op jit(solution)/shard_map/ppermute | solution.py:396
  6.5 3.7 %collective-permute-start.1 = (f32[2,128]{1,0:T(2,128)S(1)}, f32[2,128]{1,0:T(2,128)S(1)}, u32[]{:S(2)}, u32[]{:S(2)}) collective-permute-start(f32[2,128]{1,0:T(2,128)S(1)} %pad_maximum_fusion.1), channel_id=1, source_target_pairs={{0,8},{4,12},{8,0},{12,4},{16,24},{20,28},{24,16},{28,20},{1,9},{5... | collective-permute-start | bytes 3080 | tf_op jit(solution)/shard_map/ppermute | solution.py:404
  10.2 5.8 %collective-permute-start.2 = (f32[4,128]{1,0:T(4,128)S(1)}, f32[4,128]{1,0:T(4,128)S(1)}, u32[]{:S(2)}, u32[]{:S(2)}) collective-permute-start(f32[4,128]{1,0:T(4,128)S(1)} %pad_maximum_fusion.beam_ref), channel_id=1, source_target_pairs={{0,16},{4,20},{8,24},{12,28},{16,0},{20,4},{24,8},{28,12},{1,17},{... | collective-permute-start | bytes 6152 | tf_op jit(solution)/shard_map/ppermute | solution.py:404
  14.3 1.7 %copy-start.1 = (bf16[512,256]{1,0:T(8,128)(2,1)S(1)}, bf16[512,256]{1,0:T(8,128)(2,1)}, u32[]{:S(2)}) copy-start(bf16[512,256]{1,0:T(8,128)(2,1)} %constant.8.clone.spread_cols) | copy-start | bytes 786436

commit v7 on v6

--- a/solution.py
+++ b/solution.py
@@ -187,7 +187,7 @@
     lower = jnp.where(lane < HALF, 1.0, 0.0).astype(bf16)
     upper = jnp.where(lane < HALF, 0.0, 1.0).astype(bf16)
     cos_fit = fit(lambda t: np.cos(np.sqrt(t)), MIDDLE**2, 4)
-    sin_fit = fit(lambda t: np.sinc(np.sqrt(t) / np.pi), MIDDLE**2, 4)
+    sin_fit = fit(lambda t: np.sinc(np.sqrt(t) / np.pi), MIDDLE**2, 3)
     outs = ((cos_0, sin_0), (cos_1, sin_1))
     tables = []
     at = 0
@@ -315,20 +315,27 @@
     start,
 ):
     expand_wave(common_wave(plan, beam_ref, half_wave[...]), start)
-    count = plan.phase_rows[0] * ROWS
-    waves = []
-    for group in range(plan.groups):
-        at = slice(group * count, (group + 1) * count)
-        waves.append(turn(start[0], start[1], cos_0[at], sin_0[at]))
-    rows = [spread_rows(wave, plan.phase_rows[1]) for wave in waves]
-    wave = column_product(jnp.concatenate(rows, axis=0), spread_cols[...])
-    count = plan.phase_rows[1] * ROWS
-    waves = []
-    for group in range(plan.groups):
-        at = slice(group * count, (group + 1) * count)
-        waves.append(turn(wave[at, :LANES], wave[at, LANES:], cos_1[at], sin_1[at]))
-    rows = [spread_rows(wave, plan.take_rows) for wave in waves]
-    wave = column_product(jnp.concatenate(rows, axis=0), spread_cols[...])
+    parts = [range(first, first + 1) for first in range(0, plan.groups, 1)]
+    middles = []
+    for part in parts:
+        count = plan.phase_rows[0] * ROWS
+        rows = []
+        for group in part:
+            at = slice(group * count, (group + 1) * count)
+            wave = turn(start[0], start[1], cos_0[at], sin_0[at])
+            rows.append(spread_rows(wave, plan.phase_rows[1]))
+        middles.append(column_product(jnp.concatenate(rows, axis=0), spread_cols[...]))
+    finals = []
+    for part, middle in zip(parts, middles):
+        count = plan.phase_rows[1] * ROWS
+        rows = []
+        for group in part:
+            at = slice(group * count, (group + 1) * count)
+            here = slice((group - part[0]) * count, (group - part[0] + 1) * count)
+            wave = turn(middle[here, :LANES], middle[here, LANES:], cos_1[at], sin_1[at])
+            rows.append(spread_rows(wave, plan.take_rows))
+        finals += rows
+    wave = column_product(jnp.concatenate(finals, axis=0), spread_cols[...])
     lane = lax.broadcasted_iota(jnp.int32, (ROWS, LANES), 1)
     blocks = []
     count = plan.take_rows * ROWS

time: 17.9 us -> 17.9 us (level)
  no operation moved by 1% of the time
where the time goes in v7:
time: 17.9 us; the launch traced here: 17.7 us
  starting transfers between devices  10.7 us (60%)
  Pallas kernels  3.45 us (19%)
  waiting for transfers between devices  1.65 us (9%)
  local copies, waits for them, and re-layouts  1.12 us (6%)
  between operations  0.75 us (4%)
    ppermute x3, starting transfers between devices, window(): lax.ppermute(known, 'beam', [(i, i ^ reach) for i in range(beam_parts)])  8.66 us
    ppermute x2, starting transfers between devices, pass_on(): return lax.ppermute(rows, ('beam', 'tile'), pairs)  2 us
    pallas_call x1, Pallas kernels, window(): call(other, wave, cos_0, sin_0, cos_1, sin_1, jnp.asarray(column_spread()))  1.76 us
    pallas_call x1, Pallas kernels, window(): call(places, top, bottom, far, near, table, known)  1.65 us
    ppermute x3, waiting for transfers between devices, window(): lax.ppermute(known, 'beam', [(i, i ^ reach) for i in range(beam_parts)])  1.64 us
    slice x1, local copies, waits for them, and re-layouts, window(): top, bottom = (atom_counts[:, :PAD], atom_counts[:, strip_rows - PAD:])  1.09 us
  transfers between devices with their start and end apart: 5, of which 2 were waited for; matrix products, arithmetic and copies ran while one was open for 1% of the time, Pallas kernels for 9%

profile of v7, /device:TPU:0, one launch (start us, length us, event | category | flops | bytes accessed | tf_op | source)
XLA Modules:
  0.0 17.7 jit_solution(11682273582240234504)
XLA Ops:
  0.0 0.0 copy-start.2
  0.0 0.0 copy-start.3
  0.0 1.1 %fusion.1 = (bf16[2,16,4096]{2,1,0:T(8,128)(2,1)S(1)}, bf16[2,16,4096]{2,1,0:T(8,128)(2,1)S(1)}) fusion(bf16[2,32,4096]{2,1,0:T(8,128)(2,1)} %param.7), kind=kLoop, calls=%fused_computation.5 | loop fusion | bytes 1048576 | tf_op jit(solution)/shard_map/slice | solution.py:377
  1.1 0.0 copy-start
  1.1 0.0 copy-done.2
  1.1 0.0 copy-done.3
  1.2 0.0 copy-start.4
  1.2 0.5 %collective-permute-start.3 = (bf16[2,16,4096]{2,1,0:T(8,128)(2,1)S(1)}, bf16[2,16,4096]{2,1,0:T(8,128)(2,1)S(1)}, u32[]{:S(2)}, u32[]{:S(2)}) collective-permute-start(bf16[2,16,4096]{2,1,0:T(8,128)(2,1)S(1)} %get-tuple-element.14), channel_id=1, source_target_pairs={{0,1},{1,2},{2,3},{3,0},{4,5},{5,6},{6,7},{7,4},{8,9},{9,10},{10,1... | collective-permute-start | bytes 786440 | tf_op jit(solution)/shard_map/ppermute | solution.py:403
  2.4 0.0 copy-done.4
  2.4 0.1 fusion
  2.5 2.5 %collective-permute-start = (f32[1,128]{1,0:T(1,128)S(1)}, f32[1,128]{1,0:T(1,128)S(1)}, u32[]{:S(2)}, u32[]{:S(2)}) collective-permute-start(f32[1,128]{1,0:T(1,128)S(1)} %fusion), channel_id=1, source_target_pairs={{0,4},{4,0},{8,12},{12,8},{16,20},{20,16},{24,28},{28,24},{1,5},{5... | collective-permute-start | bytes 1544 | tf_op jit(solution)/shard_map/ppermute | solution.py:411
  5.0 1.5 %collective-permute-start.4 = (bf16[2,8,4096]{2,1,0:T(8,128)(2,1)S(1)}, bf16[2,8,4096]{2,1,0:T(8,128)(2,1)S(1)}, u32[]{:S(2)}, u32[]{:S(2)}) collective-permute-start(bf16[2,8,4096]{2,1,0:T(8,128)(2,1)S(1)} %get-tuple-element.15), channel_id=1, source_target_pairs={{0,3},{1,0},{2,1},{3,2},{4,7},{5,4},{6,5},{7,6},{8,11},{9,8},{10,9... | collective-permute-start | bytes 393224 | tf_op jit(solution)/shard_map/ppermute | solution.py:403
  6.4 0.1 collective-permute-done
  6.5 2.1 %collective-permute-start.1 = (f32[2,128]{1,0:T(2,128)S(1)}, f32[2,128]{1,0:T(2,128)S(1)}, u32[]{:S(2)}, u32[]{:S(2)}) collective-permute-start(f32[2,128]{1,0:T(2,128)S(1)} %pad_maximum_fusion.1), channel_id=1, source_target_pairs={{0,8},{4,12},{8,0},{12,4},{16,24},{20,28},{24,16},{28,20},{1,9},{5... | collective-permute-start | bytes 3080 | tf_op jit(solution)/shard_map/ppermute | solution.py:411
  8.6 1.6 %collective-permute-done.1 = f32[2,128]{1,0:T(2,128)S(1)} collective-permute-done((f32[2,128]{1,0:T(2,128)S(1)}, f32[2,128]{1,0:T(2,128)S(1)}, u32[]{:S(2)}, u32[]{:S(2)}) %collective-permute-start.1) | collective-permute-done | bytes 1056 | tf_op jit(solution)/shard_map/ppermute | solution.py:411
  10.2 4.1 %collective-permute-start.2 = (f32[4,128]{1,0:T(4,128)S(1)}, f32[4,128]{1,0:T(4,128)S(1)}, u32[]{:S(2)}, u32[]{:S(2)}) collective-permute-start(f32[4,128]{1,0:T(4,128)S(1)} %pad_maximum_fusion.beam_ref), channel_id=1, source_target_pairs={{0,16},{4,20},{8,24},{12,28},{16,0},{20,4},{24,8},{28,12},{1,17},{... | collective-permute-start | bytes 6152 | tf_op jit(solution)/shard_map/ppermute | solution.py:411
  14.3 0.0 collective-permute-done.4.near_ref
  14.3 0.0 collective-permute-done.3.far_ref
  14.3 0.0 copy-done
  14.3 0.0 copy-start.1
  14.3 1.6 %phases.1 = (f32[704,128]{1,0:T(8,128)S(1)}, f32[704,128]{1,0:T(8,128)S(1)}, f32[384,128]{1,0:T(8,128)S(1)}, f32[384,128]{1,0:T(8,128)S(1)}, f32[24,128]{1,0:T(8,128)S(1)}) custom-call(s32[8,64]{1,0:T(8,128)S(1)} %get-tuple-element.13.found_ref, bf16[2,16,4096]{2,1,0:T(8,128)(2,1)S(1)} %get-tuple-element.22.top_ref, ...), custom_call_target="tpu_custom_call" | custom-call | tf_op jit(solution)/shard_map/phases/pallas_call | solution.py:430
  15.9 0.0 collective-permute-done.2.beam_ref
  16.0 0.0 copy-done.1
  16.0 1.8 %finish.1 = f32[32,64]{1,0:T(8,128)} custom-call(f32[4,128]{1,0:T(4,128)S(1)} %collective-permute-done.2.beam_ref, f32[24,128]{1,0:T(8,128)S(1)} %get-tuple-element.16.half_wave, f32[704,128]{1,0:T(8,128)S(1)} %get-tuple-element.17.cos_0, f32[704,128]{1,0:T(8,128)S(1)} %get-tuple-element.18.sin_0, f32[384,128]{1,0:T(8,128)S(1)} %get-tuple-element.19.cos_1, ...), custom_call_target="tpu_custom_call" | custom-call | tf_op jit(solution)/shard_map/finish/pallas_call | solution.py:442
  (4 shorter events, 0.1 us)
Async XLA Ops:
  0.0 1.1 %copy-start.2 = (s32[64]{0:T(128)S(1)}, s32[64]{0:T(128)}, u32[]{:S(2)}) copy-start(s32[64]{0:T(128)} %param.10) | copy-start | bytes 772
  0.0 1.1 %copy-start.3 = (s32[64]{0:T(128)S(1)}, s32[64]{0:T(128)}, u32[]{:S(2)}) copy-start(s32[64]{0:T(128)} %param.11) | copy-start | bytes 772
  1.1 13.2 %copy-start = (bf16[800,256]{1,0:T(8,128)(2,1)S(1)}, bf16[800,256]{1,0:T(8,128)(2,1)}, u32[]{:S(2)}) copy-start(bf16[800,256]{1,0:T(8,128)(2,1)} %constant.7.clone.table_ref) | copy-start | bytes 1228804
  1.2 1.2 %copy-start.4 = (s32[1,2]{1,0:T(1,128)S(1)}, s32[1,2]{1,0:T(1,128)}, u32[]{:S(2)}) copy-start(s32[1,2]{1,0:T(1,128)} %param.8) | copy-start | bytes 28
  1.2 13.1 %collective-permute-start.3 = (bf16[2,16,4096]{2,1,0:T(8,128)(2,1)S(1)}, bf16[2,16,4096]{2,1,0:T(8,128)(2,1)S(1)}, u32[]{:S(2)}, u32[]{:S(2)}) collective-permute-start(bf16[2,16,4096]{2,1,0:T(8,128)(2,1)S(1)} %get-tuple-element.14), channel_id=1, source_target_pairs={{0,1},{1,2},{2,3},{3,0},{4,5},{5,6},{6,7},{7,4},{8,9},{9,10},{10,1... | collective-permute-start | bytes 786440 | tf_op jit(solution)/shard_map/ppermute | solution.py:403
  2.5 4.0 %collective-permute-start = (f32[1,128]{1,0:T(1,128)S(1)}, f32[1,128]{1,0:T(1,128)S(1)}, u32[]{:S(2)}, u32[]{:S(2)}) collective-permute-start(f32[1,128]{1,0:T(1,128)S(1)} %fusion), channel_id=1, source_target_pairs={{0,4},{4,0},{8,12},{12,8},{16,20},{20,16},{24,28},{28,24},{1,5},{5... | collective-permute-start | bytes 1544 | tf_op jit(solution)/shard_map/ppermute | solution.py:411
  5.0 9.3 %collective-permute-start.4 = (bf16[2,8,4096]{2,1,0:T(8,128)(2,1)S(1)}, bf16[2,8,4096]{2,1,0:T(8,128)(2,1)S(1)}, u32[]{:S(2)}, u32[]{:S(2)}) collective-permute-start(bf16[2,8,4096]{2,1,0:T(8,128)(2,1)S(1)} %get-tuple-element.15), channel_id=1, source_target_pairs={{0,3},{1,0},{2,1},{3,2},{4,7},{5,4},{6,5},{7,6},{8,11},{9,8},{10,9... | collective-permute-start | bytes 393224 | tf_op jit(solution)/shard_map/ppermute | solution.py:403
  6.5 3.7 %collective-permute-start.1 = (f32[2,128]{1,0:T(2,128)S(1)}, f32[2,128]{1,0:T(2,128)S(1)}, u32[]{:S(2)}, u32[]{:S(2)}) collective-permute-start(f32[2,128]{1,0:T(2,128)S(1)} %pad_maximum_fusion.1), channel_id=1, source_target_pairs={{0,8},{4,12},{8,0},{12,4},{16,24},{20,28},{24,16},{28,20},{1,9},{5... | collective-permute-start | bytes 3080 | tf_op jit(solution)/shard_map/ppermute | solution.py:411
  10.2 5.7 %collective-permute-start.2 = (f32[4,128]{1,0:T(4,128)S(1)}, f32[4,128]{1,0:T(4,128)S(1)}, u32[]{:S(2)}, u32[]{:S(2)}) collective-permute-start(f32[4,128]{1,0:T(4,128)S(1)} %pad_maximum_fusion.beam_ref), channel_id=1, source_target_pairs={{0,16},{4,20},{8,24},{12,28},{16,0},{20,4},{24,8},{28,12},{1,17},{... | collective-permute-start | bytes 6152 | tf_op jit(solution)/shard_map/ppermute | solution.py:411
  14.3 1.7 %copy-start.1 = (bf16[512,256]{1,0:T(8,128)(2,1)S(1)}, bf16[512,256]{1,0:T(8,128)(2,1)}, u32[]{:S(2)}) copy-start(bf16[512,256]{1,0:T(8,128)(2,1)} %constant.8.clone.spread_cols) | copy-start | bytes 786436
